TPU v7x, 128 devices: a whole 4x4x4 slice. The times are simulated.
128 devices in a mesh: band: 64 (over z, y, x), head: 2 (over core).
Axes of the slice: x: 4, y: 4, z: 4, core: 2. Of those that a mesh axis runs over, the one named last changes fastest.
Arguments:
- grid_state: bfloat16 [262144, 100], P('band'), may hold values from -6 to 6
- hidden_state: bfloat16 [65536, 1024], P('band', 'head'), may hold values from -6 to 6
- encoder_sources: int32 [65536, 32], P('band'), may hold values from 0 to 12287, as said below
- encoder_counts: int32 [65536], P('band'), may hold values from 1 to 32
- decoder_sources: int32 [262144, 4], P('band'), may hold values from 0 to 65535, as said below
- decoder_counts: int32 [262144], P('band'), may hold values from 1 to 4
- encoder_keys: bfloat16 [100, 1024], P(None, 'head'), may hold values from -0.625 to 0.625
- encoder_values: bfloat16 [100, 1024], P(None, 'head'), may hold values from -0.625 to 0.625
- encoder_query: bfloat16 [1024, 1024], P(None, 'head'), may hold values from -0.1875 to 0.1875
- encoder_output: bfloat16 [1024, 1024], P('head'), may hold values from -0.1875 to 0.1875
- window_query: bfloat16 [1024, 1024], P(None, 'head'), may hold values from -0.1875 to 0.1875
- window_keys: bfloat16 [1024, 1024], P(None, 'head'), may hold values from -0.1875 to 0.1875
- window_values: bfloat16 [1024, 1024], P(None, 'head'), may hold values from -0.1875 to 0.1875
- window_output: bfloat16 [1024, 1024], P('head'), may hold values from -0.1875 to 0.1875
- feed_up: bfloat16 [1024, 4096], P(None, 'head'), may hold values from -0.1875 to 0.1875
- feed_down: bfloat16 [4096, 1024], P('head'), may hold values from -0.09375 to 0.09375
- decoder_query: bfloat16 [100, 1024], P(None, 'head'), may hold values from -0.625 to 0.625
- decoder_keys: bfloat16 [1024, 1024], P(None, 'head'), may hold values from -0.1875 to 0.1875
- decoder_values: bfloat16 [1024, 1024], P(None, 'head'), may hold values from -0.1875 to 0.1875
- decoder_output: bfloat16 [1024, 100], P('head'), may hold values from -0.1875 to 0.1875
Outputs:
- grid_next: bfloat16 [262144, 100], P(('band', 'head'))
- hidden_final: bfloat16 [65536, 1024], P('band', 'head')
Inputs may be any that keep to these rules, and one draw needn't show every extreme that they name: Grid band c holds the grid points c * 4096 to (c + 1) * 4096 - 1 and hidden band c the hidden nodes c * 1024 to (c + 1) * 1024 - 1; slot e of hidden node n names the grid point (n // 1024 - 1) * 4096 + encoder_sources[n, e], which lies in a band that exists. Only the first encoder_counts[n] slots are edges. `decoder_sources`: every slot of grid point g names a hidden node of the bands g // 4096 - 1 to g // 4096 + 1 that exist. Only the first decoder_counts[g] slots are edges.
All inputs are finite; a program needn't handle non-finite values.
Results may differ from a plain program's by a relative error of at most 0.015.
Values may be sent and summed in bfloat16 or wider, within the bound.
A program may use at most 320 MiB of HBM per device.

v0:
```python
import jax
import jax.numpy as jnp
from jax import lax
from jax.sharding import PartitionSpec as P

HALF_WIN = 560
HEAD_DIM = 64


EPSILON = 1e-05
NEGATIVE = -1e30


def with_halo(cells, sides, width):
    for axis, dim in sides:
        count = lax.axis_size(axis)
        ends = count - 1
        head = lax.slice_in_dim(cells, 0, width, axis=dim)
        tail = lax.slice_in_dim(cells, cells.shape[dim] - width, cells.shape[dim], axis=dim)
        cells = jnp.concatenate(
            [
                lax.ppermute(tail, axis, [(i, (i + 1) % count) for i in range(ends)]),
                cells,
                lax.ppermute(head, axis, [((i + 1) % count, i) for i in range(ends)]),
            ],
            axis=dim,
        )
    return cells


def in_order(blocks, dim):
    blocks = jnp.moveaxis(blocks, 0, dim)
    lengths = blocks.shape
    return blocks.reshape(*lengths[:dim], lengths[dim] * lengths[dim + 1], *lengths[dim + 2 :])


def from_everyone(x, axis):
    count = lax.axis_size(axis)
    return lax.all_to_all(jnp.broadcast_to(x[None], (count, *x.shape)), axis, 0, 0, tiled=True)


def gathered_copies(x, axis, dim):
    return in_order(from_everyone(x, axis), dim)


def split_up(x, dim, count):
    lengths = x.shape
    blocks = x.reshape(*lengths[:dim], count, lengths[dim] // count, *lengths[dim + 1 :])
    return jnp.moveaxis(blocks, dim, 0)


def sent_and_summed(x, axis, dim):
    blocks = split_up(x, dim, lax.axis_size(axis))
    arrived = lax.all_to_all(blocks, axis, split_axis=0, concat_axis=0, tiled=True)
    return arrived.astype(jnp.float32).sum(axis=0)


def layer_norm(matrix):
    as_float = matrix.astype(jnp.float32)
    centred = as_float - jnp.mean(as_float, axis=-1, keepdims=True)
    variance = jnp.mean(centred * centred, axis=-1, keepdims=True)
    return (centred * lax.rsqrt(variance + EPSILON)).astype(jnp.bfloat16)


def project(matrix, weight):
    return jnp.dot(matrix, weight, preferred_element_type=jnp.float32).astype(jnp.bfloat16)


def softmax_weights(scores):
    powers = jnp.exp(scores)
    return (powers / jnp.sum(powers, axis=-1, keepdims=True)).astype(jnp.bfloat16)


def edge_attention(query, gathered, counts):
    row_count, slot_count, double_width = gathered.shape
    full_width = double_width // 2
    head_count = full_width // HEAD_DIM
    query_heads = query.reshape(row_count, head_count, HEAD_DIM)
    key_heads = gathered[:, :, :full_width].reshape(row_count, slot_count, head_count, HEAD_DIM)
    value_heads = gathered[:, :, full_width:].reshape(row_count, slot_count, head_count, HEAD_DIM)
    scores = jnp.einsum(
        "rhd,rehd->rhe", query_heads, key_heads, preferred_element_type=jnp.float32
    ) * HEAD_DIM ** (-0.5)
    slot_live = jnp.arange(slot_count, dtype=jnp.int32)[None, None, :] < counts[:, None, None]
    weights = softmax_weights(jnp.where(slot_live, scores, NEGATIVE))
    mixed = jnp.einsum("rhe,rehd->rhd", weights, value_heads, preferred_element_type=jnp.float32)
    return mixed.reshape(row_count, full_width).astype(jnp.bfloat16)


def slot_attention(query, table, sources, counts):
    row_count, full_width = query.shape
    head_count = full_width // HEAD_DIM
    query_heads = query.astype(jnp.float32).reshape(row_count, head_count, HEAD_DIM)
    slot_count = sources.shape[1]
    value_list = []
    power_list = []
    for slot in range(slot_count):
        picked = jnp.take(table, sources[:, slot], axis=0)
        key_heads = (
            picked[:, :full_width].astype(jnp.float32).reshape(row_count, head_count, HEAD_DIM)
        )
        value_list.append(picked[:, full_width:])
        score = jnp.sum(query_heads * key_heads, axis=-1) * HEAD_DIM ** (-0.5)
        score = jnp.where((slot < counts)[:, None], score, NEGATIVE)
        power_list.append(jnp.exp(score))
    total = power_list[0]
    for slot in range(1, slot_count):
        total = total + power_list[slot]
    mixed = jnp.zeros((row_count, head_count, HEAD_DIM), jnp.float32)
    for slot in range(slot_count):
        weight = (power_list[slot] / total).astype(jnp.bfloat16).astype(jnp.float32)
        value_heads = value_list[slot].astype(jnp.float32).reshape(row_count, head_count, HEAD_DIM)
        mixed = mixed + weight[:, :, None] * value_heads
    return mixed.reshape(row_count, full_width).astype(jnp.bfloat16)


def window_attention(query, pairs, live):
    query_count, full_width = query.shape
    span_count = pairs.shape[0]
    head_count = full_width // HEAD_DIM
    query_heads = query.reshape(query_count, head_count, HEAD_DIM)
    key_heads = pairs[:, :full_width].reshape(span_count, head_count, HEAD_DIM)
    value_heads = pairs[:, full_width:].reshape(span_count, head_count, HEAD_DIM)
    scores = jnp.einsum(
        "qhd,shd->hqs", query_heads, key_heads, preferred_element_type=jnp.float32
    ) * HEAD_DIM ** (-0.5)
    weights = softmax_weights(jnp.where(live[None], scores, NEGATIVE))
    mixed = jnp.einsum("hqs,shd->qhd", weights, value_heads, preferred_element_type=jnp.float32)
    return mixed.reshape(query_count, full_width).astype(jnp.bfloat16)


def local(
    grid_state,
    hidden_state,
    encoder_sources,
    encoder_counts,
    decoder_sources,
    decoder_counts,
    encoder_keys,
    encoder_values,
    encoder_query,
    encoder_output,
    window_query,
    window_keys,
    window_values,
    window_output,
    feed_up,
    feed_down,
    decoder_query,
    decoder_keys,
    decoder_values,
    decoder_output,
):
    band_index = lax.axis_index("band")
    grid_count = grid_state.shape[0]
    node_count = hidden_state.shape[0]
    grid_pair_weight = jnp.concatenate((encoder_keys, encoder_values), axis=1)
    near_grid = with_halo(grid_state, (("band", 0),), grid_count)
    near_grid_pairs = project(near_grid, grid_pair_weight)
    whole_state = gathered_copies(hidden_state, "head", 1)
    enc_query = project(layer_norm(whole_state), encoder_query)
    enc_mix = edge_attention(
        enc_query, jnp.take(near_grid_pairs, encoder_sources, axis=0), encoder_counts
    )
    enc_update = sent_and_summed(
        jnp.dot(enc_mix, encoder_output, preferred_element_type=jnp.float32).astype(jnp.bfloat16),
        "head",
        1,
    )
    hidden_mid = (hidden_state.astype(jnp.float32) + enc_update).astype(jnp.bfloat16)
    whole_mid = gathered_copies(hidden_mid, "head", 1)
    normed_mid = layer_norm(whole_mid)
    win_query = project(normed_mid, window_query)
    win_pairs = project(normed_mid, jnp.concatenate((window_keys, window_values), axis=1))
    padded_pairs = with_halo(win_pairs, (("band", 0),), HALF_WIN)
    total_nodes = node_count * lax.axis_size("band")
    first_node = band_index * node_count
    block_rows = min(512, node_count)
    span_rows = block_rows + 2 * HALF_WIN

    def attend(start):
        block_query = lax.dynamic_slice_in_dim(win_query, start, block_rows, 0)
        block_pairs = lax.dynamic_slice_in_dim(padded_pairs, start, span_rows, 0)
        query_pos = first_node + start + jnp.arange(block_rows, dtype=jnp.int32)
        key_pos = first_node + start - HALF_WIN + jnp.arange(span_rows, dtype=jnp.int32)
        distance = jnp.abs(query_pos[:, None] - key_pos[None, :])
        live = (distance <= HALF_WIN) & (key_pos[None, :] >= 0) & (key_pos[None, :] < total_nodes)
        return window_attention(block_query, block_pairs, live)

    starts = jnp.arange(node_count // block_rows, dtype=jnp.int32) * block_rows
    win_mix = lax.map(attend, starts).reshape(node_count, win_query.shape[1])
    win_update = sent_and_summed(
        jnp.dot(win_mix, window_output, preferred_element_type=jnp.float32).astype(jnp.bfloat16),
        "head",
        1,
    )
    hidden_att = (hidden_mid.astype(jnp.float32) + win_update).astype(jnp.bfloat16)
    whole_att = gathered_copies(hidden_att, "head", 1)
    inner = jax.nn.gelu(
        jnp.dot(layer_norm(whole_att), feed_up, preferred_element_type=jnp.float32),
        approximate=True,
    ).astype(jnp.bfloat16)
    feed_update = sent_and_summed(
        jnp.dot(inner, feed_down, preferred_element_type=jnp.float32).astype(jnp.bfloat16),
        "head",
        1,
    )
    hidden_final = (hidden_att.astype(jnp.float32) + feed_update).astype(jnp.bfloat16)
    whole_final = gathered_copies(hidden_final, "head", 1)
    query_weight, key_weight, value_weight, out_weight = (
        decoder_query,
        decoder_keys,
        decoder_values,
        decoder_output,
    )
    own_grid, own_sources, own_counts = (grid_state, decoder_sources, decoder_counts)
    node_pair_weight = jnp.concatenate((key_weight, value_weight), axis=1)
    near_final = with_halo(whole_final, (("band", 0),), node_count)
    near_node_pairs = project(layer_norm(near_final), node_pair_weight)
    node_local = own_sources - (band_index - 1) * node_count
    dec_query = project(own_grid, query_weight)
    dec_mix = slot_attention(dec_query, near_node_pairs, node_local, own_counts)
    dec_terms = jnp.dot(dec_mix, out_weight, preferred_element_type=jnp.float32)
    dec_update = sent_and_summed(dec_terms.astype(jnp.bfloat16), "head", 0)
    part_count = dec_update.shape[0]
    part_grid = lax.dynamic_slice_in_dim(
        grid_state, lax.axis_index("head") * part_count, part_count, 0
    )
    grid_next = (part_grid.astype(jnp.float32) + dec_update).astype(jnp.bfloat16)
    return (grid_next, hidden_final)


def solution(mesh):
    in_specs = (
        P("band", None),
        P("band", "head"),
        P("band", None),
        P("band"),
        P("band", None),
        P("band"),
        P(None, "head"),
        P(None, "head"),
        P(None, "head"),
        P("head", None),
        P(None, "head"),
        P(None, "head"),
        P(None, "head"),
        P("head", None),
        P(None, "head"),
        P("head", None),
        P(None, "head"),
        P(None, "head"),
        P(None, "head"),
        P("head", None),
    )
    out_specs = (P(("band", "head"), None), P("band", "head"))
    return jax.shard_map(local, mesh=mesh, in_specs=in_specs, out_specs=out_specs, check_vma=False)
```

profile of v0, /device:TPU:97, one launch (start us, length us, event | category | flops | bytes accessed | tf_op | source)
XLA Modules:
  0.0 877.0 jit_solution(1702216552559940822)
XLA Ops:
  0.6 6.8 collective-permute-start.1
  26.4 7.0 collective-permute-done
  33.5 13.6 %convolution_convert_fusion = bf16[12288,1024]{1,0:T(8,128)(2,1)} fusion(bf16[4096,100]{0,1:T(8,128)(2,1)} %collective-permute-done.1, bf16[4096,100]{0,1:T(8,128)(2,1)S(1)} %copy-done.9, bf16[4096,100]{0,1:T(8,128)(2,1)} %collective-permute-done, bf16[100,512]{1,0:T(8,128)(2,1)S(1)} %copy-done.15, bf16[100,512]{1,0:T(8,128)(2,1)S(1)} %copy-done.16), kind=kOutput, calls=%fused_computation.26 | convolution fusion | flops 2536947712 | bytes 27828224 | tf_op jit(solution)/shard_map/dot_general | solution.py:66
  47.0 170.6 %gather_fusion = bf16[32768,1024]{1,0:T(8,128)(2,1)} fusion(bf16[12288,1024]{1,0:T(8,128)(2,1)} %convolution_convert_fusion, s32[32768]{0:T(1024)S(1)} %broadcast_clamp_fusion), kind=kCustom, calls=%fused_computation.4 | custom fusion | bytes 134348800 | tf_op jit(solution)/shard_map/jit(_take)/gather | solution.py:163
  217.6 89.0 %copy.58 = bf16[1024,32,1024]{0,2,1:T(8,128)(2,1)} copy(bf16[1024,32,1024]{2,1,0:T(8,128)(2,1)} %bitcast.12) | data formatting | bytes 134217728 | tf_op jit(solution)/shard_map/jit(_take)/gather | solution.py:163
  306.6 44.7 %broadcast_select_fusion = bf16[1024,32,1024]{0,2,1:T(8,128)(2,1)} fusion(bf16[1024,32,1024]{0,2,1:T(8,128)(2,1)} %copy.58, pred[1024,32]{0,1:T(8,128)(4,1)S(1)} %copy-done.14), kind=kLoop, calls=%fused_computation.25 | loop fusion | flops 33554432 | bytes 134250496 | tf_op jit(solution)/shard_map/jit(_take)/select_n | solution.py:163
  351.4 45.0 %fusion.89 = (bf16[1024,32,512]{0,2,1:T(8,128)(2,1)}, bf16[1024,32,512]{0,2,1:T(8,128)(2,1)}) fusion(bf16[1024,32,1024]{0,2,1:T(8,128)(2,1)} %broadcast_select_fusion), kind=kLoop, calls=%fused_computation.178 | loop fusion | bytes 134217728 | tf_op jit(solution)/shard_map/slice | solution.py:79
  396.4 11.7 %multiply_reduce_fusion.1 = f32[1024,8,32]{0,1,2:T(8,128)S(1)} fusion(f32[1024,8,64]{0,2,1:T(8,128)S(1)} %copy-done.8, bf16[1024,32,512]{0,2,1:T(8,128)(2,1)} %get-tuple-element.133), kind=kLoop, calls=%fused_computation.24 | loop fusion | flops 50069504 | bytes 36700160
  409.7 12.7 %multiply_reduce_fusion = bf16[1024,8,64]{0,2,1:T(8,128)(2,1)S(1)} fusion(bf16[1024,8,32,64]{0,3,1,2:T(8,128)(2,1)} %bitcast.126, f32[1024,8,32]{0,1,2:T(8,128)S(1)} %copy.86), kind=kLoop, calls=%fused_computation.23 | loop fusion | flops 49807360 | bytes 35651584 | tf_op jit(solution)/shard_map/rhe,rehd->rhd/dot_general | solution.py:86
  423.7 7.0 all_to_all.40
  450.9 20.1 %collective-permute-done.3 = bf16[560,1024]{1,0:T(8,128)(2,1)S(1)} collective-permute-done((bf16[560,1024]{1,0:T(8,128)(2,1)S(1)}, bf16[560,1024]{1,0:T(8,128)(2,1)S(1)}, u32[]{:S(2)}, u32[]{:S(2)}) %collective-permute-start.3) | collective-permute-done | bytes 1146912 | tf_op jit(solution)/shard_map/ppermute | solution.py:24
  480.1 90.3 %while.12 = (s32[]{:T(128)}, bf16[2,512,512]{2,1,0:T(8,128)(2,1)}, s32[2]{0:T(128)}, bf16[2144,1024]{1,0:T(8,128)(2,1)}, s32[]{:T(128)}, /*index=5*/bf16[1024,51...) while((s32[]{:T(128)}, bf16[2,512,512]{2,1,0:T(8,128)(2,1)}, ...), condition=%wide.region_8.9_spmd, body=%wide.region_6.8_spmd.sunk | while | flops 1762511744 | bytes 93068752 | solution.py:191
  498.4 13.6 %fusion.125 = (f32[8,512]{1,0:T(8,128)S(1)}, f32[8,512,1632]{1,2,0:T(8,128)}) fusion(pred[512,1632]{0,1:T(8,128)(4,1)S(1)} %fusion.124, bf16[512,8,64]{0,2,1:T(8,128)(2,1)S(1)} %bitcast.134, bf16[1632,8,64]{0,2,1:T(8,128)(2,1)} %bitcast.128), kind=kOutput, calls=%fused_computation.7.clone.1 | convolution fusion | flops 875687936 | bytes 29786112 | tf_op jit(solution)/shard_map/while/body/eval_jaxpr/qhd,shd->hqs/dot_general | solution.py:124
  512.0 11.9 %fusion.126 = bf16[8,64,512]{2,1,0:T(8,128)(2,1)S(1)} fusion(bf16[1632,8,64]{0,2,1:T(8,128)(2,1)S(1)} %bitcast.127, f32[8,512,1632]{1,2,0:T(8,128)} %get-tuple-element.199, f32[8,512]{1,0:T(8,128)S(1)} %get-tuple-element.200, pred[512,1632]{0,1:T(8,128)(4,1)S(1)} %fusion.124), kind=kOutput, calls=%fused_computation.12.clone.1 | convolution fusion | flops 882638848 | bytes 29786112 | tf_op jit(solution)/shard_map/while/body/eval_jaxpr/hqs,shd->qhd/dot_general | solution.py:128
  543.6 13.6 %fusion.125 = (f32[8,512]{1,0:T(8,128)S(1)}, f32[8,512,1632]{1,2,0:T(8,128)}) fusion(pred[512,1632]{0,1:T(8,128)(4,1)S(1)} %fusion.124, bf16[512,8,64]{0,2,1:T(8,128)(2,1)S(1)} %bitcast.134, bf16[1632,8,64]{0,2,1:T(8,128)(2,1)} %bitcast.128), kind=kOutput, calls=%fused_computation.7.clone.1 | convolution fusion | flops 875687936 | bytes 29786112 | tf_op jit(solution)/shard_map/while/body/eval_jaxpr/qhd,shd->hqs/dot_general | solution.py:124
  557.2 11.9 %fusion.126 = bf16[8,64,512]{2,1,0:T(8,128)(2,1)S(1)} fusion(bf16[1632,8,64]{0,2,1:T(8,128)(2,1)S(1)} %bitcast.127, f32[8,512,1632]{1,2,0:T(8,128)} %get-tuple-element.199, f32[8,512]{1,0:T(8,128)S(1)} %get-tuple-element.200, pred[512,1632]{0,1:T(8,128)(4,1)S(1)} %fusion.124), kind=kOutput, calls=%fused_computation.12.clone.1 | convolution fusion | flops 882638848 | bytes 29786112 | tf_op jit(solution)/shard_map/while/body/eval_jaxpr/hqs,shd->qhd/dot_general | solution.py:128
  589.3 15.6 %fusion.56 = bf16[1024,1024]{0,1:T(8,128)(2,1)} fusion(bf16[2048,1024]{1,0:T(8,128)(2,1)} %param.39, bf16[1024,1024]{0,1:T(8,128)(2,1)} %fusion.34, bf16[1024,2048]{1,0:T(8,128)(2,1)} %param.38), kind=kOutput, calls=%fused_computation.107 | convolution fusion | flops 8609857536 | bytes 12582912 | tf_op jit(solution)/shard_map/dot_general | solution.py:204
  604.9 6.6 all_to_all.44
  625.2 41.7 %collective-permute-done.5 = bf16[1024,1024]{0,1:T(8,128)(2,1)} collective-permute-done((bf16[1024,1024]{0,1:T(8,128)(2,1)S(1)}, bf16[1024,1024]{0,1:T(8,128)(2,1)}, u32[]{:S(2)}, u32[]{:S(2)}) %collective-permute-start.5) | collective-permute-done | bytes 2097184 | tf_op jit(solution)/shard_map/ppermute | solution.py:24
  680.5 12.1 %fusion.30 = bf16[3072,1024]{1,0:T(8,128)(2,1)} fusion(f32[3072]{0:T(1024)S(1)} %add_rsqrt_fusion, f32[3072]{0:T(1024)S(1)} %broadcast_multiply_fusion, bf16[1024,512]{1,0:T(8,128)(2,1)S(1)} %copy-done.26, bf16[1024,512]{1,0:T(8,128)(2,1)S(1)} %copy-done.27, bf16[1024,1024]{0,1:T(8,128)(2,1)} %collective-permute-done.5, ...), kind=kOutput, calls=%fused_computation.67 | convolution fusion | flops 6478102528 | bytes 14704640 | tf_op jit(solution)/shard_map/dot_general | solution.py:66
  692.7 24.5 %gather_fusion.4 = bf16[4096,1024]{1,0:T(8,128)(2,1)} fusion(bf16[3072,1024]{1,0:T(8,128)(2,1)} %fusion.30, s32[4096]{0:T(1024)S(1)} %fusion.79), kind=kCustom, calls=%fused_computation.3.clone | custom fusion | bytes 16793600 | tf_op jit(solution)/shard_map/jit(_take)/gather | solution.py:98
  717.1 11.3 %copy.65 = bf16[4096,1024]{0,1:T(8,128)(2,1)} copy(bf16[4096,1024]{1,0:T(8,128)(2,1)} %gather_fusion.4) | data formatting | bytes 16777216 | tf_op jit(solution)/shard_map/jit(_take)/gather | solution.py:98
  728.4 24.5 %gather_fusion.3 = bf16[4096,1024]{1,0:T(8,128)(2,1)} fusion(bf16[3072,1024]{1,0:T(8,128)(2,1)} %fusion.30, s32[4096]{0:T(1024)S(1)} %fusion.78), kind=kCustom, calls=%fused_computation.2.clone | custom fusion | bytes 16793600 | tf_op jit(solution)/shard_map/jit(_take)/gather | solution.py:98
  752.9 11.5 %copy.64 = bf16[4096,1024]{0,1:T(8,128)(2,1)} copy(bf16[4096,1024]{1,0:T(8,128)(2,1)} %gather_fusion.3) | data formatting | bytes 16777216 | tf_op jit(solution)/shard_map/jit(_take)/gather | solution.py:98
  764.4 24.5 %gather_fusion.2 = bf16[4096,1024]{1,0:T(8,128)(2,1)} fusion(bf16[3072,1024]{1,0:T(8,128)(2,1)} %fusion.30, s32[4096]{0:T(1024)S(1)} %fusion.77), kind=kCustom, calls=%fused_computation.1.clone | custom fusion | bytes 16793600 | tf_op jit(solution)/shard_map/jit(_take)/gather | solution.py:98
  788.8 11.2 %copy.63 = bf16[4096,1024]{0,1:T(8,128)(2,1)} copy(bf16[4096,1024]{1,0:T(8,128)(2,1)} %gather_fusion.2) | data formatting | bytes 16777216 | tf_op jit(solution)/shard_map/jit(_take)/gather | solution.py:98
  800.1 24.4 %gather_fusion.1 = bf16[4096,1024]{1,0:T(8,128)(2,1)} fusion(bf16[3072,1024]{1,0:T(8,128)(2,1)} %fusion.30, s32[4096]{0:T(1024)S(1)} %fusion.76), kind=kCustom, calls=%fused_computation.clone | custom fusion | bytes 16793600 | tf_op jit(solution)/shard_map/jit(_take)/gather | solution.py:98
  824.5 12.2 %copy.62 = bf16[4096,1024]{0,1:T(8,128)(2,1)} copy(bf16[4096,1024]{1,0:T(8,128)(2,1)} %gather_fusion.1) | data formatting | bytes 16777216 | tf_op jit(solution)/shard_map/jit(_take)/gather | solution.py:98
  836.8 6.8 broadcast_select_fusion.1
  845.1 9.8 %broadcast_select_fusion.3 = (bf16[4096,1024]{0,1:T(8,128)(2,1)}, bf16[4096,1024]{0,1:T(8,128)(2,1)}) fusion(bf16[4096,1024]{0,1:T(8,128)(2,1)} %copy.63, pred[4096]{0:T(1024)(128)(4,1)S(1)} %compare_and_fusion.3, bf16[4096,1024]{0,1:T(8,128)(2,1)S(1)} %copy-done.3, pred[4096]{0:T(1024)(128)(4,1)S(1)} %compare_and_fusion.4), kind=kLoop, calls=%fused_computation.60 | loop fusion | flops 8388608 | bytes 33562624 | tf_op jit(solution)/shard_map/jit(_take)/select_n | solution.py:98
  854.9 6.9 bitcast_reduce_fusion
  862.1 6.6 fusion.23
  (173 shorter events, 137.9 us)
Async XLA Ops:
  0.6 421.8 %copy-start = (bf16[512,1024]{1,0:T(8,128)(2,1)S(1)}, bf16[512,1024]{1,0:T(8,128)(2,1)}, u32[]{:S(2)}) copy-start(bf16[512,1024]{1,0:T(8,128)(2,1)} %param.33) | copy-start | bytes 3145732
  0.6 25.8 %collective-permute-start.1 = (bf16[4096,100]{0,1:T(8,128)(2,1)}, bf16[4096,100]{0,1:T(8,128)(2,1)}, u32[]{:S(2)}, u32[]{:S(2)}) collective-permute-start(bf16[4096,100]{0,1:T(8,128)(2,1)} %param.24), channel_id=1, source_target_pairs={{2,0},{4,2},{6,4},{8,6},{10,8},{12,10},{14,12},{16,14},{18,16},{20... | collective-permute-start | bytes 2457608 | tf_op jit(solution)/shard_map/ppermute | solution.py:24
  7.5 26.0 %collective-permute-start = (bf16[4096,100]{0,1:T(8,128)(2,1)}, bf16[4096,100]{0,1:T(8,128)(2,1)}, u32[]{:S(2)}, u32[]{:S(2)}) collective-permute-start(bf16[4096,100]{0,1:T(8,128)(2,1)} %param.24), channel_id=1, source_target_pairs={{0,2},{2,4},{4,6},{6,8},{8,10},{10,12},{12,14},{14,16},{16,18},{18... | collective-permute-start | bytes 2457608 | tf_op jit(solution)/shard_map/ppermute | solution.py:22
  10.9 7.1 copy-start.12
  12.6 9.3 %copy-start.21 = (s32[1024]{0:T(1024)S(1)}, s32[1024]{0:T(1024)}, u32[]{:S(2)}) copy-start(s32[1024]{0:T(1024)} %param.27) | copy-start | bytes 12292
  12.6 8.3 all-to-all-start
  23.7 9.7 %copy-start.9 = (bf16[4096,100]{0,1:T(8,128)(2,1)S(1)}, bf16[4096,100]{0,1:T(8,128)(2,1)}, u32[]{:S(2)}) copy-start(bf16[4096,100]{0,1:T(8,128)(2,1)} %param.24) | copy-start | bytes 2457604
  23.7 9.7 %copy-start.15 = (bf16[100,512]{1,0:T(8,128)(2,1)S(1)}, bf16[100,512]{1,0:T(8,128)(2,1)}, u32[]{:S(2)}) copy-start(bf16[100,512]{1,0:T(8,128)(2,1)} %param.31) | copy-start | bytes 307204
  23.7 9.7 %copy-start.16 = (bf16[100,512]{1,0:T(8,128)(2,1)S(1)}, bf16[100,512]{1,0:T(8,128)(2,1)}, u32[]{:S(2)}) copy-start(bf16[100,512]{1,0:T(8,128)(2,1)} %param.30) | copy-start | bytes 307204
  217.6 89.0 %copy-start.14 = (pred[1024,32]{0,1:T(8,128)(4,1)S(1)}, pred[1024,32]{0,1:T(8,128)(4,1)}, u32[]{:S(2)}) copy-start(pred[1024,32]{0,1:T(8,128)(4,1)} %compare_and_fusion) | copy-start | bytes 98308
  351.4 45.0 %copy-start.8 = (f32[1024,8,64]{0,2,1:T(8,128)S(1)}, f32[1024,8,64]{0,2,1:T(8,128)}, u32[]{:S(2)}) copy-start(f32[1024,8,64]{0,2,1:T(8,128)} %bitcast_convert_fusion) | copy-start | bytes 6291460
  396.4 11.8 %copy-start.19 = (pred[1024,32]{0,1:T(8,128)(4,1)S(1)}, pred[1024,32]{0,1:T(8,128)(4,1)}, u32[]{:S(2)}) copy-start(pred[1024,32]{0,1:T(8,128)(4,1)} %iota_compare_fusion) | copy-start | bytes 98308
  423.7 7.5 copy-start.5
  442.4 5.7 copy-start.18
  442.4 6.3 copy-start.25
  442.6 28.5 %collective-permute-start.3 = (bf16[560,1024]{1,0:T(8,128)(2,1)S(1)}, bf16[560,1024]{1,0:T(8,128)(2,1)S(1)}, u32[]{:S(2)}, u32[]{:S(2)}) collective-permute-start(bf16[560,1024]{1,0:T(8,128)(2,1)S(1)} %get-tuple-element.136), channel_id=1, source_target_pairs={{2,0},{4,2},{6,4},{8,6},{10,8},{12,10},{14,12},{16,14},{18,16},{20... | collective-permute-start | bytes 3440648 | tf_op jit(solution)/shard_map/ppermute | solution.py:24
  444.7 32.6 %collective-permute-start.2 = (bf16[560,1024]{1,0:T(8,128)(2,1)S(1)}, bf16[560,1024]{1,0:T(8,128)(2,1)S(1)}, u32[]{:S(2)}, u32[]{:S(2)}) collective-permute-start(bf16[560,1024]{1,0:T(8,128)(2,1)S(1)} %get-tuple-element.135), channel_id=1, source_target_pairs={{0,2},{2,4},{4,6},{6,8},{8,10},{10,12},{12,14},{14,16},{16,18},{18... | collective-permute-start | bytes 3440648 | tf_op jit(solution)/shard_map/ppermute | solution.py:22
  498.4 13.6 %copy-start.2 = (bf16[1632,512]{0,1:T(8,128)(2,1)S(1)}, bf16[1632,512]{0,1:T(8,128)(2,1)}, u32[]{:S(2)}) copy-start(bf16[1632,512]{0,1:T(8,128)(2,1)} %copy.102) | copy-start | bytes 5013508 | tf_op jit(solution)/shard_map/while
  512.0 12.2 %copy-start.28 = (bf16[2,512,512]{2,1,0:T(8,128)(2,1)S(1)}, bf16[2,512,512]{2,1,0:T(8,128)(2,1)}, u32[]{:S(2)}) copy-start(bf16[2,512,512]{2,1,0:T(8,128)(2,1)} %get-tuple-element.214) | copy-start | bytes 3145732 | tf_op jit(solution)/shard_map/while
  543.6 13.6 %copy-start.2 = (bf16[1632,512]{0,1:T(8,128)(2,1)S(1)}, bf16[1632,512]{0,1:T(8,128)(2,1)}, u32[]{:S(2)}) copy-start(bf16[1632,512]{0,1:T(8,128)(2,1)} %copy.102) | copy-start | bytes 5013508 | tf_op jit(solution)/shard_map/while
  557.2 12.2 %copy-start.28 = (bf16[2,512,512]{2,1,0:T(8,128)(2,1)S(1)}, bf16[2,512,512]{2,1,0:T(8,128)(2,1)}, u32[]{:S(2)}) copy-start(bf16[2,512,512]{2,1,0:T(8,128)(2,1)} %get-tuple-element.214) | copy-start | bytes 3145732 | tf_op jit(solution)/shard_map/while
  573.2 6.9 copy-start.7
  612.4 11.0 %copy-start.13 = (s32[4096,4]{0,1:T(4,128)S(1)}, s32[4096,4]{0,1:T(4,128)}, u32[]{:S(2)}) copy-start(s32[4096,4]{0,1:T(4,128)} %broadcast_subtract_fusion) | copy-start | bytes 196612
  612.4 11.2 %copy-start.20 = (s32[4096]{0:T(1024)S(1)}, s32[4096]{0:T(1024)}, u32[]{:S(2)}) copy-start(s32[4096]{0:T(1024)} %param.29) | copy-start | bytes 49156
  618.1 48.8 %collective-permute-start.5 = (bf16[1024,1024]{0,1:T(8,128)(2,1)S(1)}, bf16[1024,1024]{0,1:T(8,128)(2,1)}, u32[]{:S(2)}, u32[]{:S(2)}) collective-permute-start(bf16[1024,1024]{0,1:T(8,128)(2,1)S(1)} %bitcast.129), channel_id=1, source_target_pairs={{2,0},{4,2},{6,4},{8,6},{10,8},{12,10},{14,12},{16,14},{18,16},{20... | collective-permute-start | bytes 6291464 | tf_op jit(solution)/shard_map/ppermute | solution.py:24
  620.0 53.0 %collective-permute-start.4 = (bf16[1024,1024]{0,1:T(8,128)(2,1)S(1)}, bf16[1024,1024]{0,1:T(8,128)(2,1)}, u32[]{:S(2)}, u32[]{:S(2)}) collective-permute-start(bf16[1024,1024]{0,1:T(8,128)(2,1)S(1)} %bitcast.130), channel_id=1, source_target_pairs={{0,2},{2,4},{4,6},{6,8},{8,10},{10,12},{12,14},{14,16},{16,18},{18... | collective-permute-start | bytes 6291464 | tf_op jit(solution)/shard_map/ppermute | solution.py:22
  836.8 8.3 copy-start.3
  845.1 9.8 %copy-start.10 = (bf16[4096,100]{0,1:T(8,128)(2,1)S(1)}, bf16[4096,100]{0,1:T(8,128)(2,1)}, u32[]{:S(2)}) copy-start(bf16[4096,100]{0,1:T(8,128)(2,1)} %param.24) | copy-start | bytes 2457604
  845.1 9.8 %copy-start.30 = (bf16[100,512]{1,0:T(8,128)(2,1)S(1)}, bf16[100,512]{1,0:T(8,128)(2,1)}, u32[]{:S(2)}) copy-start(bf16[100,512]{1,0:T(8,128)(2,1)} %param.40) | copy-start | bytes 307204
  862.1 6.7 copy-start.17
  868.8 7.8 copy-start.1
  870.0 5.7 copy-start.11
  (9 other events, 17.2 us)
where the time goes:
time: 885 us; the launch traced here: 877 us
  local copies, waits for them, and re-layouts  490 us (55%)
  other arithmetic  119 us (13%)
  matrix products  112 us (13%)
  waiting for transfers between devices  81.2 us (9%)
  blocking collectives  41.7 us (5%)
  starting transfers between devices  24.3 us (3%)
    gather x2, local copies, waits for them, and re-layouts, local(): jnp.take(near_grid_pairs, encoder_sources, axis=0)  260 us
    gather x8, local copies, waits for them, and re-layouts, slot_attention(): picked = jnp.take(table, sources[:, slot], axis=0)  144 us
    ppermute x3, waiting for transfers between devices, with_halo(): lax.ppermute(head, axis, [((i + 1) % count, i) for i in range(ends)])  61.9 us
    slice x1, local copies, waits for them, and re-layouts, edge_attention(): gathered[:, :, :full_width]  45 us
    select_n x2, other arithmetic, local(): jnp.take(near_grid_pairs, encoder_sources, axis=0)  44.7 us
    dot_general x6, matrix products, project(): jnp.dot(matrix, weight, preferred_element_type=jnp.float32)  40 us
    dot_general x2, matrix products, window_attention(): jnp.einsum('qhd,shd->hqs', query_heads, key_heads, preferred_element_type...  27.2 us
    all_to_all x4, blocking collectives, sent_and_summed(): lax.all_to_all(blocks, axis, split_axis=0, concat_axis=0, tiled=True)  25.3 us
  transfers between devices with their start and end apart: 7, of which 5 were waited for; matrix products, arithmetic and copies ran while one was open for 2% of the time, Pallas kernels for 0%

commit v1 on v0

v1 whole, which is shorter than its diff:
```python
import functools

import jax
import jax.numpy as jnp
from jax import lax
from jax.experimental import pallas as pl
from jax.experimental.pallas import tpu as pltpu
from jax.sharding import PartitionSpec as P

HALF_WIN = 560
HEAD_DIM = 64
EPSILON = 1e-05
NEGATIVE = -1e30
SCALE = HEAD_DIM**-0.5
MESH = pl.DeviceIdType.MESH
NB = 16
QB = 128
GB = 64
RB = 256
ANY = pl.BlockSpec(memory_space=pl.ANY)
VM = pl.BlockSpec(memory_space=pltpu.VMEM)


def layer_norm(matrix):
    as_float = matrix.astype(jnp.float32)
    centred = as_float - jnp.mean(as_float, axis=-1, keepdims=True)
    variance = jnp.mean(centred * centred, axis=-1, keepdims=True)
    return (centred * lax.rsqrt(variance + EPSILON)).astype(jnp.bfloat16)


def project(matrix, weight):
    return jnp.dot(matrix, weight, preferred_element_type=jnp.float32).astype(jnp.bfloat16)


def places():
    band = lax.axis_index("band")
    head = lax.axis_index("head")
    count = lax.axis_size("band")
    left = lax.rem(band + count - 1, count)
    right = lax.rem(band + 1, count)
    return band, head, left, right


def greet(others):
    barrier = pltpu.get_barrier_semaphore()
    for other in others:
        pl.semaphore_signal(barrier, inc=1, device_id=other, device_id_type=MESH)
    pl.semaphore_wait(barrier, len(others))


class Sender:
    def __init__(self, send_sem, recv_sem):
        self.send_sem, self.recv_sem, self.used, self.open = send_sem, recv_sem, 0, []

    def send(self, src, dst, device):
        n = self.used
        self.used += 1
        copy = pltpu.make_async_remote_copy(
            src_ref=src, dst_ref=dst, send_sem=self.send_sem.at[n], recv_sem=self.recv_sem.at[n],
            device_id=device, device_id_type=MESH)
        copy.start()
        self.open.append(copy)
        return copy

    def finish(self, received=()):
        for copy in self.open:
            copy.wait_send()
            if not any(copy is other for other in received):
                copy.wait_recv()


def half_of(ref, dim, index):
    size = ref.shape[dim] // 2
    part = pl.ds(pl.multiple_of(index * size, size), size)
    return ref.at[part] if dim == 0 else ref.at[:, part]


def relay(near, source, width, sides, sender, me, band, left, right, head, chunks):
    step = width // 2 // chunks
    waves = []
    for c in range(chunks):
        own = pl.ds(pl.multiple_of(head * (width // 2) + c * step, step), step)
        for side, other in ((sides[0], right), (sides[1], left)):
            rows = pl.ds(pl.multiple_of(side * width + head * (width // 2) + c * step, step), step)
            waves.append((sender.send(source(own, c, step), near.at[rows], (other, head)), rows))
    return waves


def start_kernel(n_pair, dims, *refs):
    grid, state = refs[0], refs[1]
    halves = refs[2 : 2 + n_pair]
    near, whole = refs[2 + n_pair], refs[3 + n_pair]
    fulls = refs[4 + n_pair : 4 + 2 * n_pair]
    rest = refs[4 + 2 * n_pair :]
    state_hold = rest[0]
    holds = rest[1 : 1 + n_pair]
    send_sem, recv_sem, load_sem, store_sem = rest[1 + n_pair :]
    band, head, left, right = places()
    peer = (band, 1 - head)
    loads = [pltpu.make_async_copy(half_of(state, 0, head), state_hold, load_sem.at[n_pair])]
    loads += [pltpu.make_async_copy(h, v, load_sem.at[n]) for n, (h, v) in enumerate(zip(halves, holds))]
    for load in loads:
        load.start()
    greet([peer, (left, head), (right, head)])
    sender = Sender(send_sem, recv_sem)
    waves = relay(near, lambda own, c, step: grid.at[own], grid.shape[0], (0, 1), sender, None, band, left, right, head, 4)
    sender.send(half_of(state, 0, 1 - head), half_of(whole, 1, head), peer)
    for n in range(n_pair):
        sender.send(halves[n], half_of(fulls[n], dims[n], head), peer)
    stores = [pltpu.make_async_copy(state_hold, half_of(whole, 1, head), store_sem.at[n_pair])]
    stores += [pltpu.make_async_copy(holds[n], half_of(fulls[n], dims[n], head), store_sem.at[n]) for n in range(n_pair)]
    for load, store in zip(loads, stores):
        load.wait()
        store.start()
    for copy, rows in waves:
        copy.wait_recv()
        sender.send(near.at[rows], near.at[rows], peer)
    sender.finish([copy for copy, _ in waves])
    for store in stores:
        store.wait()


def full_shape(half, dim):
    shape = list(half.shape)
    shape[dim] *= 2
    return jax.ShapeDtypeStruct(tuple(shape), half.dtype)


def start_exchange(grid, state, pairs):
    halves = [half for half, _ in pairs]
    dims = [dim for _, dim in pairs]
    n = len(pairs)
    nodes, width = state.shape
    outs = [jax.ShapeDtypeStruct((2 * grid.shape[0], grid.shape[1]), grid.dtype),
            jax.ShapeDtypeStruct((nodes // 2, width * 2), state.dtype)]
    outs += [full_shape(half, dim) for half, dim in pairs]
    copies = 16 + 1 + n
    return pl.pallas_call(
        functools.partial(start_kernel, n, dims),
        out_shape=outs,
        in_specs=[VM] + [ANY] * (n + 1),
        out_specs=[ANY] * (n + 2),
        scratch_shapes=[pltpu.VMEM((nodes // 2, width), state.dtype)]
        + [pltpu.VMEM(half.shape, half.dtype) for half in halves]
        + [pltpu.SemaphoreType.DMA((copies,))] * 2
        + [pltpu.SemaphoreType.DMA((n + 1,))] * 2,
        compiler_params=pltpu.CompilerParams(collective_id=0, has_side_effects=True, vmem_limit_bytes=32 << 20),
        name="start_exchange",
    )(grid, state, *halves)


def window_kernel_exchange(n_pair, dims, *refs):
    rows = refs[0]
    halves = refs[1 : 1 + n_pair]
    span = refs[1 + n_pair]
    fulls = refs[2 + n_pair : 2 + 2 * n_pair]
    rest = refs[2 + 2 * n_pair :]
    holds = rest[:n_pair]
    send_sem, recv_sem, load_sem, store_sem = rest[n_pair:]
    band, head, left, right = places()
    count = rows.shape[0]
    extra = HALF_WIN - count
    after = HALF_WIN + count
    peer = (band, 1 - head)
    across = (lax.rem(band + lax.axis_size("band") + 2 * head - 1, lax.axis_size("band")), 1 - head)
    loads = [pltpu.make_async_copy(h, v, load_sem.at[n]) for n, (h, v) in enumerate(zip(halves, holds))]
    for load in loads:
        load.start()
    own = pltpu.make_async_copy(rows, span.at[pl.ds(HALF_WIN, count)], store_sem.at[n_pair])
    own.start()
    greet([peer, (left, head), (right, head), across])
    sender = Sender(send_sem, recv_sem)
    sender.send(rows, span.at[pl.ds(pl.multiple_of(after + head * (extra - after), 16), count)], across)
    sender.send(rows.at[pl.ds(count - extra, extra)], span.at[pl.ds(0, extra)], (right, head))
    sender.send(rows.at[pl.ds(0, extra)], span.at[pl.ds(after + count, extra)], (left, head))
    sender.send(rows, span.at[pl.ds(pl.multiple_of(extra + head * (after - extra), 16), count)], peer)
    for n in range(n_pair):
        sender.send(halves[n], half_of(fulls[n], dims[n], head), peer)
    stores = [pltpu.make_async_copy(holds[n], half_of(fulls[n], dims[n], head), store_sem.at[n]) for n in range(n_pair)]
    for load, store in zip(loads, stores):
        load.wait()
        store.start()
    sender.finish()
    own.wait()
    for store in stores:
        store.wait()


def window_exchange(rows, span_rows, pairs):
    halves = [half for half, _ in pairs]
    dims = [dim for _, dim in pairs]
    n = len(pairs)
    outs = [jax.ShapeDtypeStruct((span_rows, rows.shape[1]), rows.dtype)]
    outs += [full_shape(half, dim) for half, dim in pairs]
    copies = 4 + n
    return pl.pallas_call(
        functools.partial(window_kernel_exchange, n, dims),
        out_shape=outs,
        in_specs=[VM] + [ANY] * n,
        out_specs=[ANY] * (n + 1),
        scratch_shapes=[pltpu.VMEM(half.shape, half.dtype) for half in halves]
        + [pltpu.SemaphoreType.DMA((copies,))] * 2
        + [pltpu.SemaphoreType.DMA((n + 1,))] * 2,
        compiler_params=pltpu.CompilerParams(collective_id=1, has_side_effects=True, vmem_limit_bytes=32 << 20),
        name="window_exchange",
    )(rows, *halves)


def final_kernel_exchange(n_pair, dims, *refs):
    rows = refs[0]
    halves = refs[1 : 1 + n_pair]
    near = refs[1 + n_pair]
    fulls = refs[2 + n_pair : 2 + 2 * n_pair]
    rest = refs[2 + 2 * n_pair :]
    holds = rest[:n_pair]
    send_sem, recv_sem, load_sem, store_sem = rest[n_pair:]
    band, head, left, right = places()
    count = rows.shape[0]
    peer = (band, 1 - head)
    loads = [pltpu.make_async_copy(h, v, load_sem.at[n]) for n, (h, v) in enumerate(zip(halves, holds))]
    for load in loads:
        load.start()
    mine = pl.ds(pl.multiple_of(2 * count + head * count, count), count)
    own = pltpu.make_async_copy(rows, near.at[mine], store_sem.at[n_pair])
    own.start()
    greet([peer, (left, head), (right, head)])
    sender = Sender(send_sem, recv_sem)
    waves = relay(near, lambda o, c, step: rows.at[pl.ds(c * step, step)], 2 * count, (0, 2), sender, None, band, left, right, head, 4)
    sender.send(rows, near.at[mine], peer)
    for n in range(n_pair):
        sender.send(halves[n], half_of(fulls[n], dims[n], head), peer)
    stores = [pltpu.make_async_copy(holds[n], half_of(fulls[n], dims[n], head), store_sem.at[n]) for n in range(n_pair)]
    for load, store in zip(loads, stores):
        load.wait()
        store.start()
    for copy, place in waves:
        copy.wait_recv()
        sender.send(near.at[place], near.at[place], peer)
    sender.finish([copy for copy, _ in waves])
    own.wait()
    for store in stores:
        store.wait()


def final_exchange(rows, pairs):
    halves = [half for half, _ in pairs]
    dims = [dim for _, dim in pairs]
    n = len(pairs)
    outs = [jax.ShapeDtypeStruct((6 * rows.shape[0], rows.shape[1]), rows.dtype)]
    outs += [full_shape(half, dim) for half, dim in pairs]
    copies = 16 + 1 + n
    return pl.pallas_call(
        functools.partial(final_kernel_exchange, n, dims),
        out_shape=outs,
        in_specs=[VM] + [ANY] * n,
        out_specs=[ANY] * (n + 1),
        scratch_shapes=[pltpu.VMEM(half.shape, half.dtype) for half in halves]
        + [pltpu.SemaphoreType.DMA((copies,))] * 2
        + [pltpu.SemaphoreType.DMA((n + 1,))] * 2,
        compiler_params=pltpu.CompilerParams(collective_id=2, has_side_effects=True, vmem_limit_bytes=32 << 20),
        name="final_exchange",
    )(rows, *halves)


E_ENC = 32
E_DEC = 4


def enc_kernel(idx, q, wk, wv, go, near, bias, out, table, g, qk, mg):
    i = pl.program_id(0)
    steps = pl.num_programs(0)
    nodes = q.shape[0]
    heads2 = q.shape[1] // 128
    lane = lax.broadcasted_iota(jnp.int32, (1, 128), 1)
    low = lane < 64

    @pl.when(i == 0)
    def _():
        band = go.shape[0]
        for part, ref in enumerate((near.at[0:band], go, near.at[band:])):
            @pl.loop(0, band // 128)
            def _(b):
                r = pl.multiple_of(b * 128, 128)
                table[pl.ds(part * band + r, 128), 0, :] = ref[pl.ds(r, 128), :].astype(jnp.float32)
        for c in range(heads2):
            qc = q[:, c * 128:(c + 1) * 128].astype(jnp.float32)
            wc = wk[:, c * 128:(c + 1) * 128]
            for par in range(2):
                qm = jnp.where(low if par == 0 else ~low, qc, 0.0).astype(jnp.bfloat16)
                r = lax.dot_general(qm, wc, (((1,), (1,)), ((), ())), preferred_element_type=jnp.float32)
                qk[2 * c + par] = (r * SCALE).astype(jnp.bfloat16)

    rows = NB * E_ENC
    for r in range(rows):
        g[r:r + 1, :] = table[idx[i * rows + r]]
    gb = g[...].astype(jnp.bfloat16)
    n0 = pl.multiple_of(i * NB, NB)
    qb = qk[:, pl.ds(n0, NB), :].reshape(heads2 * 2 * NB, 128)
    s = lax.dot_general(qb, gb, (((1,), (1,)), ((), ())), preferred_element_type=jnp.float32)
    rn = lax.broadcasted_iota(jnp.int32, s.shape, 0) % NB
    cn = lax.broadcasted_iota(jnp.int32, s.shape, 1) // E_ENC
    s = jnp.where(rn == cn, s + bias[0], NEGATIVE)
    p = jnp.exp(s)
    l = jnp.sum(p, axis=-1, keepdims=True)
    m = jnp.dot(p.astype(jnp.bfloat16), gb, preferred_element_type=jnp.float32) / l
    mg[:, pl.ds(n0, NB), :] = m.astype(jnp.bfloat16).reshape(heads2 * 2, NB, 128)

    @pl.when(i == steps - 1)
    def _():
        for c in range(heads2):
            wc = wv[:, c * 128:(c + 1) * 128]
            a = jnp.dot(mg[2 * c], wc, preferred_element_type=jnp.float32)
            b = jnp.dot(mg[2 * c + 1], wc, preferred_element_type=jnp.float32)
            out[:, c * 128:(c + 1) * 128] = jnp.where(low, a, b).astype(jnp.bfloat16)

def enc_attention(q, wk, wv, go, near, sources, counts):
    nodes, width = q.shape
    slots = sources.shape[1]
    steps = nodes // NB
    live = jnp.arange(slots, dtype=jnp.int32)[None, :] < counts[:, None]
    bias = jnp.where(live, 0.0, NEGATIVE).astype(jnp.float32).reshape(steps, 1, NB * slots)
    full = lambda a: pl.BlockSpec(a.shape, lambda i, s: (0,) * a.ndim, pipeline_mode=pl.Buffered(1))
    return pl.pallas_call(
        enc_kernel,
        out_shape=jax.ShapeDtypeStruct((nodes, width), jnp.bfloat16),
        grid_spec=pltpu.PrefetchScalarGridSpec(
            num_scalar_prefetch=1, grid=(steps,),
            in_specs=[full(q), full(wk), full(wv), full(go), full(near),
                      pl.BlockSpec((1, 1, NB * slots), lambda i, s: (i, 0, 0))],
            out_specs=pl.BlockSpec((nodes, width), lambda i, s: (0, 0)),
            scratch_shapes=[
                pltpu.VMEM((3 * go.shape[0], 1, 128), jnp.float32),
                pltpu.VMEM((NB * slots, 128), jnp.float32),
                pltpu.VMEM((width // 64, nodes, 128), jnp.bfloat16),
                pltpu.VMEM((width // 64, nodes, 128), jnp.bfloat16)]),
        compiler_params=pltpu.CompilerParams(dimension_semantics=("arbitrary",), vmem_limit_bytes=48 << 20),
        cost_estimate=pl.CostEstimate(flops=4 << 30, bytes_accessed=8 << 20, transcendentals=4 << 20),
        name="enc_attention",
    )(sources.reshape(-1), q, wk, wv, go, near, bias)


def win_kernel(q, k, v, ones, out, p):
    nodes = q.shape[0]
    span = p.shape[-1]
    lane = lax.broadcasted_iota(jnp.int32, (1, 128), 1)
    low = lane < 64
    for b in range(nodes // QB):
        s0 = b * QB
        kb = k[s0:s0 + span, :]
        ve = jnp.concatenate((v[s0:s0 + span, :], ones[s0:s0 + span, :]), axis=1)
        qc = q[s0:s0 + QB, :].astype(jnp.float32) * SCALE
        res = []
        for par in range(2):
            qm = jnp.where(low if par == 0 else ~low, qc, 0.0).astype(jnp.bfloat16)
            for t in range(0, span, 256):
                w = min(256, span - t)
                s = lax.dot_general(qm, kb[t:t + w, :], (((1,), (1,)), ((), ())), preferred_element_type=jnp.float32)
                e = jnp.exp(s)
                if t < QB or t + w - 1 > 2 * HALF_WIN:
                    d = lax.broadcasted_iota(jnp.int32, s.shape, 1) + t - lax.broadcasted_iota(jnp.int32, s.shape, 0)
                    e = jnp.where((d >= 0) & (d <= 2 * HALF_WIN), e, 0.0)
                p[2*b+par, :, t:t + w] = e.astype(jnp.bfloat16)
            o = jnp.dot(p[2*b+par], ve, preferred_element_type=jnp.float32)
            res.append(o[:, :128] / o[:, 128:])
        out[s0:s0 + QB, :] = jnp.where(low, res[0], res[1]).astype(jnp.bfloat16)

def window(q, k, v, ones):
    nodes, width = q.shape
    span = -(-(QB + 2 * HALF_WIN) // 128) * 128
    keys = k.shape[0]
    return pl.pallas_call(
        win_kernel, out_shape=jax.ShapeDtypeStruct((nodes, width), jnp.bfloat16),
        grid=(width // 128,),
        in_specs=[pl.BlockSpec((nodes, 128), lambda c: (0, c)), pl.BlockSpec((keys, 128), lambda c: (0, c)),
                  pl.BlockSpec((keys, 128), lambda c: (0, c)), pl.BlockSpec((keys, 128), lambda c: (0, 0))],
        out_specs=pl.BlockSpec((nodes, 128), lambda c: (0, c)),
        scratch_shapes=[pltpu.VMEM((2*nodes//QB, QB, span), jnp.bfloat16)],
        compiler_params=pltpu.CompilerParams(dimension_semantics=("arbitrary",), vmem_limit_bytes=48 << 20),
        name="window_attention")(q, k, v, ones)


def dec_kernel(idx, cnt, x, wk, wv, gs, wq, wo, out, table, q3, prod, sc, mix3, seg):
    i = pl.program_id(0)
    tsteps = table.shape[0] // RB
    lane = lax.broadcasted_iota(jnp.int32, (1, 128), 1)

    @pl.when(i == 0)
    def _():
        r = lax.broadcasted_iota(jnp.int32, (128, 128), 0) // 64
        c = lax.broadcasted_iota(jnp.int32, (128, 128), 1) // 64
        seg[...] = jnp.where(r == c, 1.0, 0.0).astype(jnp.bfloat16)

    @pl.when(i < tsteps)
    def _():
        xf = x[...].astype(jnp.float32)
        cen = xf - jnp.mean(xf, axis=-1, keepdims=True)
        var = jnp.mean(cen * cen, axis=-1, keepdims=True)
        xn = (cen * lax.rsqrt(var + EPSILON)).astype(jnp.bfloat16)
        r0 = pl.multiple_of(i * RB, RB)
        for part, w in enumerate((wk, wk, wv, wv)):
            kv = jnp.dot(xn, w[:, (part % 2) * 512:(part % 2 + 1) * 512], preferred_element_type=jnp.float32)
            for s in range(4):
                table[pl.ds(r0, RB), part * 4 + s, :] = kv[:, s * 128:(s + 1) * 128]

    @pl.when(i >= tsteps)
    def _():
        b = i - tsteps
        g0 = b * GB
        gb = gs[...]
        qf = jnp.dot(gb, wq[...], preferred_element_type=jnp.float32) * SCALE
        for s in range(8):
            q3[:, s, :] = qf[:, s * 128:(s + 1) * 128]
        for g in range(GB):
            qv = q3[g]
            for e in range(E_DEC):
                prod[e, g] = qv * table[idx[(g0 + g) * E_DEC + e], 0:8, :]
        pm = prod[...].reshape(E_DEC * GB * 8, 128).astype(jnp.bfloat16)
        sc[...] = jnp.exp(jnp.dot(pm, seg[...], preferred_element_type=jnp.float32)).reshape(E_DEC, GB, 8, 128)
        for g in range(GB):
            c = cnt[g0 + g]
            tot = None
            acc = None
            for e in range(E_DEC):
                pe = sc[e, g]
                if e > 0:
                    pe = jnp.where(e < c, pe, 0.0)
                pv = pe * table[idx[(g0 + g) * E_DEC + e], 8:16, :]
                tot = pe if e == 0 else tot + pe
                acc = pv if e == 0 else acc + pv
            mix3[g] = acc / tot
        o = gb.astype(jnp.float32)
        m2 = jnp.concatenate([mix3[:, s, :] for s in range(8)], axis=1).astype(jnp.bfloat16)
        o = o + jnp.dot(m2, wo[...], preferred_element_type=jnp.float32)
        out[...] = o[:, :out.shape[1]].astype(jnp.bfloat16)

def decode(x, wk, wv, gs, wq, wo, sources, counts, variables):
    rows, width = x.shape
    grid_rows = gs.shape[0]
    tsteps = rows // RB
    steps = tsteps + grid_rows // GB
    full = lambda a: pl.BlockSpec(a.shape, lambda i, *_: (0,) * a.ndim, pipeline_mode=pl.Buffered(1))
    late = lambda i, *_: (jnp.maximum(i - tsteps, 0), 0)
    return pl.pallas_call(
        dec_kernel,
        out_shape=jax.ShapeDtypeStruct((grid_rows, variables), jnp.bfloat16),
        grid_spec=pltpu.PrefetchScalarGridSpec(
            num_scalar_prefetch=2, grid=(steps,),
            in_specs=[pl.BlockSpec((RB, width), lambda i, *_: (jnp.minimum(i, tsteps - 1), 0)),
                      full(wk), full(wv),
                      pl.BlockSpec((GB, 128), late), full(wq), full(wo)],
            out_specs=pl.BlockSpec((GB, variables), late),
            scratch_shapes=[
                pltpu.VMEM((rows, 16, 128), jnp.float32),
                pltpu.VMEM((GB, 8, 128), jnp.float32),
                pltpu.VMEM((E_DEC, GB, 8, 128), jnp.float32),
                pltpu.VMEM((E_DEC, GB, 8, 128), jnp.float32),
                pltpu.VMEM((GB, 8, 128), jnp.float32),
                pltpu.VMEM((128, 128), jnp.bfloat16)]),
        compiler_params=pltpu.CompilerParams(dimension_semantics=("arbitrary",), vmem_limit_bytes=56 << 20),
        name="dec_attention",
    )(sources.reshape(-1), counts, x, wk, wv, gs, wq, wo)


def local(
    grid_state,
    hidden_state,
    encoder_sources,
    encoder_counts,
    decoder_sources,
    decoder_counts,
    encoder_keys,
    encoder_values,
    encoder_query,
    encoder_output,
    window_query,
    window_keys,
    window_values,
    window_output,
    feed_up,
    feed_down,
    decoder_query,
    decoder_keys,
    decoder_values,
    decoder_output,
):
    band, head, _, _ = places()
    bands = lax.axis_size("band")
    band_nodes, half_width = hidden_state.shape
    nodes = band_nodes // 2
    grid_count, variables = grid_state.shape
    half_grid = grid_count // 2
    short = 128 - variables
    widen = lambda w: jnp.pad(w, ((0, short), (0, 0)))
    grid = jnp.pad(grid_state, ((0, 0), (0, short)))
    near_grid, state, enc_k, enc_v, enc_q, enc_o, win_q, win_k, win_v, win_o, dec_q, dec_o = start_exchange(
        grid, hidden_state,
        [(widen(encoder_keys), 1), (widen(encoder_values), 1), (encoder_query, 1), (encoder_output, 0),
         (window_query, 1), (window_keys, 1), (window_values, 1), (window_output, 0),
         (widen(decoder_query), 1), (jnp.pad(decoder_output, ((0, 0), (0, short))), 0)],
    )
    my_rows = lambda a, size: lax.dynamic_slice_in_dim(a, head * size, size, 0)
    query = project(layer_norm(state), enc_q)
    mix = enc_attention(query, enc_k, enc_v, grid, near_grid, my_rows(encoder_sources, nodes), my_rows(encoder_counts, nodes))
    mid = (state.astype(jnp.float32) + jnp.dot(mix, enc_o, preferred_element_type=jnp.float32)).astype(jnp.bfloat16)
    normed = layer_norm(mid)
    span = nodes + 2 * HALF_WIN
    span_rows = nodes - QB + -(-(QB + 2 * HALF_WIN) // 128) * 128
    near, up, down = window_exchange(normed, span_rows, [(feed_up, 1), (feed_down, 0)])
    place = jnp.arange(span_rows, dtype=jnp.int32)
    node = band * band_nodes + head * nodes - HALF_WIN + place
    live = ((place < span) & (node >= 0) & (node < bands * band_nodes))[:, None]
    near = jnp.where(live, near, jnp.zeros_like(near))
    ones = jnp.broadcast_to(live, (span_rows, 128)).astype(jnp.bfloat16)
    mixed = window(project(normed, win_q), project(near, win_k), project(near, win_v), ones)
    att = (mid.astype(jnp.float32) + jnp.dot(mixed, win_o, preferred_element_type=jnp.float32)).astype(jnp.bfloat16)
    inner = jax.nn.gelu(
        jnp.dot(layer_norm(att), up, preferred_element_type=jnp.float32), approximate=True
    ).astype(jnp.bfloat16)
    final = (att.astype(jnp.float32) + jnp.dot(inner, down, preferred_element_type=jnp.float32)).astype(jnp.bfloat16)
    near_final, dec_k, dec_v = final_exchange(final, [(decoder_keys, 1), (decoder_values, 1)])
    hidden_final = lax.dynamic_slice(near_final, (band_nodes, head * half_width), (band_nodes, half_width))
    sources = my_rows(decoder_sources, half_grid) - (band - 1) * band_nodes
    grid_next = decode(near_final, dec_k, dec_v, my_rows(grid, half_grid), dec_q, dec_o, sources,
                       my_rows(decoder_counts, half_grid), variables)
    return (grid_next, hidden_final)


def solution(mesh):
    in_specs = (
        P("band", None),
        P("band", "head"),
        P("band", None),
        P("band"),
        P("band", None),
        P("band"),
        P(None, "head"),
        P(None, "head"),
        P(None, "head"),
        P("head", None),
        P(None, "head"),
        P(None, "head"),
        P(None, "head"),
        P("head", None),
        P(None, "head"),
        P("head", None),
        P(None, "head"),
        P(None, "head"),
        P(None, "head"),
        P("head", None),
    )
    out_specs = (P(("band", "head"), None), P("band", "head"))
    return jax.shard_map(local, mesh=mesh, in_specs=in_specs, out_specs=out_specs, check_vma=False)
```

time: 885 us -> 287 us (0.32)
  the two profiles are of different devices: /device:TPU:97 before, /device:TPU:1 now
where the time goes in v1:
time: 287 us; the launch traced here: 286 us
  Pallas kernels  216 us (75%)
  local copies, waits for them, and re-layouts  34 us (12%)
  matrix products  32.4 us (11%)
    pallas_call x1, Pallas kernels, decode(): pl.pallas_call(dec_kernel, out_shape=jax.ShapeDtypeStruct((grid_rows, var...  85.2 us
    pallas_call x1, Pallas kernels, enc_attention(): pl.pallas_call(enc_kernel, out_shape=jax.ShapeDtypeStruct((nodes, width),...  34.7 us
    pallas_call x1, Pallas kernels, final_exchange(): pl.pallas_call(functools.partial(final_kernel_exchange, n, dims), out_sha...  33 us
    pallas_call x1, Pallas kernels, start_exchange(): pl.pallas_call(functools.partial(start_kernel, n, dims), out_shape=outs,...  25.7 us
    pallas_call x1, Pallas kernels, window_exchange(): pl.pallas_call(functools.partial(window_kernel_exchange, n, dims), out_sh...  22 us
    unnamed x63, local copies, waits for them, and re-layouts  20.6 us
    pallas_call x1, Pallas kernels, window(): pl.pallas_call(win_kernel, out_shape=jax.ShapeDtypeStruct((nodes, width),...  15.8 us
    dot_general x1, matrix products, local(): jnp.dot(inner, down, preferred_element_type=jnp.float32)  15.5 us

profile of v1, /device:TPU:1, one launch (start us, length us, event | category | flops | bytes accessed | tf_op | source)
XLA Modules:
  0.0 286.4 jit_solution(7822740860613532478)
XLA Ops:
  1.5 1.3 dynamic_slice.19.cnt
  3.7 0.9 pad.19.refs_2_
  4.6 0.9 pad.20.refs_3_
  6.5 1.0 copy.27
  8.8 1.3 reshape.100.idx
  10.1 2.4 copy.26
  12.5 2.1 constant_dynamic-slice_fusion.gs
  14.6 1.4 pad.18.refs_0_.go
  16.1 1.2 copy-done.12
  17.4 1.2 copy-done.13
  18.6 25.7 %start_exchange.1 = (bf16[8192,128]{1,0:T(8,128)(2,1)S(1)}, bf16[512,1024]{1,0:T(8,128)(2,1)S(1)}, bf16[128,1024]{1,0:T(8,128)(2,1)S(1)}, bf16[128,1024]{1,0:T(8...) custom-call(bf16[4096,128]{1,0:T(8,128)(2,1)S(1)} %pad.18.refs_0_.go, ...), custom_call_target="tpu_custom_call" | custom-call | tf_op jit(solution)/shard_map/start_exchange/pallas_call | solution.py:138
  45.7 1.3 copy-done.19
  47.0 1.3 copy-done.21
  48.4 1.3 copy-done.24
  50.3 1.3 convolution_convert_fusion.3.q
  52.0 34.7 %enc_attention.1 = bf16[512,1024]{1,0:T(8,128)(2,1)S(1)} custom-call(s32[16384]{0:T(1024)S(1)} %reshape.101.idx, bf16[512,1024]{1,0:T(8,128)(2,1)S(1)} %convolution_convert_fusion.3.q, bf16[128,1024]{1,0:T(8,128)(2,1)S(1)} %get-tuple-element.22.wk, bf16[128,1024]{1,0:T(8,128)(2,1)S(1)} %get-tuple-element.23.wv, bf16[4096,128]{1,0:T(8,128)(2,1)S(1)} %pad.18.refs_0_.go, ...), custom_call_target="tpu_custom_call" | custom-call | flops 4294967296 | bytes 8388608 | tf_op jit(solution)/shard_map/enc_attention/pallas_call | solution.py:323
  86.7 3.1 %convert_reduce_fusion.1 = (f32[512]{0:T(512)S(1)}, bf16[512,1024]{1,0:T(8,128)(2,1)S(1)}) fusion(bf16[512,1024]{1,0:T(8,128)(2,1)S(1)} %enc_attention.1, bf16[1024,1024]{1,0:T(8,128)(2,1)} %copy-done.23, bf16[512,1024]{1,0:T(8,128)(2,1)S(1)} %get-tuple-element.20), kind=kOutput, calls=%fused_computation.18 | convolution fusion | flops 1076362752 | bytes 5244928 | tf_op jit(solution)/shard_map/dot_general | solution.py:504
  90.5 1.3 convolution_convert_fusion.2.q
  92.4 1.4 copy-done.3
  93.7 22.0 %window_exchange.1 = (bf16[1664,1024]{1,0:T(8,128)(2,1)S(1)}, bf16[1024,4096]{1,0:T(8,128)(2,1)S(1)}, bf16[4096,1024]{1,0:T(8,128)(2,1)}) custom-call(bf16[512,1024]{1,0:T(8,128)(2,1)S(1)} %fusion.19.refs_0_, bf16[1024,2048]{1,0:T(8,128)(2,1)S(1)} %copy-done.3, bf16[2048,1024]{1,0:T(8,128)(2,1)S(1)} %copy-done.4), custom_call_target="tpu_custom_call" | custom-call | tf_op jit(solution)/shard_map/window_exchange/pallas_call | solution.py:196
  115.8 5.5 %convolution_convert_fusion.v = bf16[1664,1024]{1,0:T(8,128)(2,1)} fusion(bf16[1024,1024]{1,0:T(8,128)(2,1)S(1)} %copy-done.29, bf16[1664,1024]{1,0:T(8,128)(2,1)S(1)} %get-tuple-element.27, pred[1664]{0:T(1024)(128)(4,1)S(1)} %get-tuple-element.46), kind=kOutput, calls=%fused_computation.10 | convolution fusion | flops 3493068800 | bytes 8914560 | tf_op jit(solution)/shard_map/dot_general | solution.py:32
  121.4 4.4 %convolution_convert_fusion.1.k = bf16[1664,1024]{1,0:T(8,128)(2,1)S(1)} fusion(bf16[1024,1024]{1,0:T(8,128)(2,1)S(1)} %copy-done.20, bf16[1664,1024]{1,0:T(8,128)(2,1)S(1)} %get-tuple-element.27, pred[1664]{0:T(1024)(128)(4,1)S(1)} %get-tuple-element.46), kind=kOutput, calls=%fused_computation.11 | convolution fusion | flops 3493068800 | bytes 8914560 | tf_op jit(solution)/shard_map/dot_general | solution.py:32
  125.7 15.8 %window_attention.1 = bf16[512,1024]{1,0:T(8,128)(2,1)S(1)} custom-call(bf16[512,1024]{1,0:T(8,128)(2,1)S(1)} %convolution_convert_fusion.2.q, bf16[1664,1024]{1,0:T(8,128)(2,1)S(1)} %convolution_convert_fusion.1.k, bf16[1664,1024]{1,0:T(8,128)(2,1)} %convolution_convert_fusion.v, bf16[1664,128]{1,0:T(8,128)(2,1)S(1)} %broadcast_in_dim.37.ones), custom_call_target="tpu_custom_call" | custom-call | tf_op jit(solution)/shard_map/window_attention/pallas_call | solution.py:371
  141.5 1.3 convert_reduce_fusion
  143.9 15.5 %fusion.24.refs_0_ = bf16[512,1024]{1,0:T(8,128)(2,1)S(1)} fusion(bf16[512,1024]{1,0:T(8,128)(2,1)} %copy-done.27, bf16[4096,1024]{1,0:T(8,128)(2,1)} %get-tuple-element.32, bf16[1024,4096]{1,0:T(8,128)(2,1)} %copy-done.18, f32[512]{0:T(512)S(1)} %add_rsqrt_fusion, f32[512]{0:T(512)S(1)} %broadcast_multiply_fusion), kind=kOutput, calls=%fused_computation.36 | convolution fusion | flops 8612478976 | bytes 18878464 | tf_op jit(solution)/shard_map/dot_general | solution.py:519
  159.4 33.0 %final_exchange.1 = (bf16[3072,1024]{1,0:T(8,128)(2,1)S(1)}, bf16[1024,1024]{1,0:T(8,128)(2,1)S(1)}, bf16[1024,1024]{1,0:T(8,128)(2,1)S(1)}) custom-call(bf16[512,1024]{1,0:T(8,128)(2,1)S(1)} %fusion.24.refs_0_, bf16[1024,512]{1,0:T(8,128)(2,1)S(1)} %copy-done.14, bf16[1024,512]{1,0:T(8,128)(2,1)S(1)} %copy-done.15), custom_call_target="tpu_custom_call" | custom-call | tf_op jit(solution)/shard_map/final_exchange/pallas_call | solution.py:252
  192.4 2.6 copy-done.2
  195.1 1.4 copy-done.5
  196.5 1.4 copy-done.6
  197.8 85.2 %dec_attention.1 = bf16[2048,100]{1,0:T(8,128)(2,1)} custom-call(s32[8192]{0:T(1024)} %reshape.100.idx, s32[2048]{0:T(1024)} %dynamic_slice.19.cnt, bf16[3072,1024]{1,0:T(8,128)(2,1)} %copy-done.2, bf16[1024,1024]{1,0:T(8,128)(2,1)} %copy-done.5, bf16[1024,1024]{1,0:T(8,128)(2,1)} %copy-done.6, bf16[2048,128]{1,0:T(8,128)(2,1)} %constant_dynamic-slice_fusion.gs, ...), custom_call_target="tpu_custom_call" | custom-call | tf_op jit(solution)/shard_map/dec_attention/pallas_call | solution.py:443
  283.0 2.3 constant_dynamic-slice_fusion.2
  285.4 1.0 copy.29
  (78 shorter events, 8.7 us)
Async XLA Ops:
  0.6 3.1 %copy-start = (s32[1024,32]{0,1:T(8,128)S(1)}, s32[1024,32]{0,1:T(8,128)}, u32[]{:S(2)}) copy-start(s32[1024,32]{0,1:T(8,128)} %param.22) | copy-start | bytes 393220
  10.1 6.0 %copy-start.10 = (bf16[1024,512]{1,0:T(8,128)(2,1)S(1)}, bf16[1024,512]{1,0:T(8,128)(2,1)}, u32[]{:S(2)}) copy-start(bf16[1024,512]{1,0:T(8,128)(2,1)} %refs_6_.1) | copy-start | bytes 3145732
  10.1 6.0 %copy-start.11 = (bf16[1024,512]{1,0:T(8,128)(2,1)S(1)}, bf16[1024,512]{1,0:T(8,128)(2,1)}, u32[]{:S(2)}) copy-start(bf16[1024,512]{1,0:T(8,128)(2,1)} %refs_7_.1) | copy-start | bytes 3145732
  12.5 3.6 %copy-start.7 = (bf16[1024,512]{1,0:T(8,128)(2,1)S(1)}, bf16[1024,512]{1,0:T(8,128)(2,1)}, u32[]{:S(2)}) copy-start(bf16[1024,512]{1,0:T(8,128)(2,1)} %refs_1_.3) | copy-start | bytes 3145732
  12.5 3.6 %copy-start.8 = (bf16[1024,512]{1,0:T(8,128)(2,1)S(1)}, bf16[1024,512]{1,0:T(8,128)(2,1)}, u32[]{:S(2)}) copy-start(bf16[1024,512]{1,0:T(8,128)(2,1)} %refs_4_.1) | copy-start | bytes 3145732
  12.5 3.6 %copy-start.9 = (bf16[512,1024]{1,0:T(8,128)(2,1)S(1)}, bf16[512,1024]{1,0:T(8,128)(2,1)}, u32[]{:S(2)}) copy-start(bf16[512,1024]{1,0:T(8,128)(2,1)} %refs_5_.1) | copy-start | bytes 3145732
  16.1 1.2 copy-start.12
  17.3 1.2 copy-start.13
  44.3 0.7 copy-start.16
  45.0 0.7 copy-start.17
  45.7 1.3 copy-start.19
  47.0 1.3 copy-start.21
  48.4 1.3 copy-start.24
  49.7 2.0 copy-start.23
  50.3 1.7 copy-start.25
  86.7 3.9 %copy-start.22 = (bf16[1024,1024]{1,0:T(8,128)(2,1)S(1)}, bf16[1024,1024]{1,0:T(8,128)(2,1)}, u32[]{:S(2)}) copy-start(bf16[1024,1024]{1,0:T(8,128)(2,1)} %copy-done.21) | copy-start | bytes 6291460
  90.2 2.2 copy-start.4
  90.5 3.2 %copy-start.3 = (bf16[1024,2048]{1,0:T(8,128)(2,1)S(1)}, bf16[1024,2048]{1,0:T(8,128)(2,1)}, u32[]{:S(2)}) copy-start(bf16[1024,2048]{1,0:T(8,128)(2,1)} %refs_1_.4) | copy-start | bytes 12582916
  93.7 22.0 %copy-start.29 = (bf16[1024,1024]{1,0:T(8,128)(2,1)S(1)}, bf16[1024,1024]{1,0:T(8,128)(2,1)}, u32[]{:S(2)}) copy-start(bf16[1024,1024]{1,0:T(8,128)(2,1)} %get-tuple-element.29) | copy-start | bytes 6291460
  115.8 5.6 %copy-start.18 = (bf16[1024,4096]{1,0:T(8,128)(2,1)}, bf16[1024,4096]{1,0:T(8,128)(2,1)S(1)}, u32[]{:S(2)}) copy-start(bf16[1024,4096]{1,0:T(8,128)(2,1)S(1)} %get-tuple-element.31) | copy-start | bytes 25165828
  115.8 5.6 %copy-start.20 = (bf16[1024,1024]{1,0:T(8,128)(2,1)S(1)}, bf16[1024,1024]{1,0:T(8,128)(2,1)}, u32[]{:S(2)}) copy-start(bf16[1024,1024]{1,0:T(8,128)(2,1)} %copy-done.19) | copy-start | bytes 6291460
  125.7 15.8 %copy-start.28 = (bf16[1024,1024]{1,0:T(8,128)(2,1)S(1)}, bf16[1024,1024]{1,0:T(8,128)(2,1)}, u32[]{:S(2)}) copy-start(bf16[1024,1024]{1,0:T(8,128)(2,1)} %get-tuple-element.30) | copy-start | bytes 6291460
  142.9 1.0 copy-start.27
  143.9 15.5 %copy-start.14 = (bf16[1024,512]{1,0:T(8,128)(2,1)S(1)}, bf16[1024,512]{1,0:T(8,128)(2,1)}, u32[]{:S(2)}) copy-start(bf16[1024,512]{1,0:T(8,128)(2,1)} %refs_1_.5) | copy-start | bytes 3145732
  143.9 15.5 %copy-start.15 = (bf16[1024,512]{1,0:T(8,128)(2,1)S(1)}, bf16[1024,512]{1,0:T(8,128)(2,1)}, u32[]{:S(2)}) copy-start(bf16[1024,512]{1,0:T(8,128)(2,1)} %refs_2_.3) | copy-start | bytes 3145732
  192.4 2.7 copy-start.2
  195.1 1.4 copy-start.5
  196.5 1.4 copy-start.6
  197.8 88.5 %copy-start.1 = (s32[1024,32]{0,1:T(8,128)S(1)}, s32[1024,32]{0,1:T(8,128)}, u32[]{:S(2)}) copy-start(s32[1024,32]{0,1:T(8,128)} %param.22) | copy-start | bytes 393220
  283.0 2.3 copy-start.26

commit v2 on v1

--- a/solution.py
+++ b/solution.py
@@ -12,12 +12,14 @@
 EPSILON = 1e-05
 NEGATIVE = -1e30
 SCALE = HEAD_DIM**-0.5
+LOG2E = 1.4426950408889634
 MESH = pl.DeviceIdType.MESH
 NB = 16
 QB = 128
-GB = 64
+GB = 128
+UN = 16
 RB = 256
-ANY = pl.BlockSpec(memory_space=pl.ANY)
+ANY = pl.BlockSpec(memory_space=pltpu.HBM)
 VM = pl.BlockSpec(memory_space=pltpu.VMEM)
 
 
@@ -144,7 +146,7 @@
         + [pltpu.VMEM(half.shape, half.dtype) for half in halves]
         + [pltpu.SemaphoreType.DMA((copies,))] * 2
         + [pltpu.SemaphoreType.DMA((n + 1,))] * 2,
-        compiler_params=pltpu.CompilerParams(collective_id=0, has_side_effects=True, vmem_limit_bytes=32 << 20),
+        compiler_params=pltpu.CompilerParams(collective_id=0, has_side_effects=True, vmem_limit_bytes=60 << 20),
         name="start_exchange",
     )(grid, state, *halves)
 
@@ -201,7 +203,7 @@
         scratch_shapes=[pltpu.VMEM(half.shape, half.dtype) for half in halves]
         + [pltpu.SemaphoreType.DMA((copies,))] * 2
         + [pltpu.SemaphoreType.DMA((n + 1,))] * 2,
-        compiler_params=pltpu.CompilerParams(collective_id=1, has_side_effects=True, vmem_limit_bytes=32 << 20),
+        compiler_params=pltpu.CompilerParams(collective_id=1, has_side_effects=True, vmem_limit_bytes=60 << 20),
         name="window_exchange",
     )(rows, *halves)
 
@@ -257,7 +259,7 @@
         scratch_shapes=[pltpu.VMEM(half.shape, half.dtype) for half in halves]
         + [pltpu.SemaphoreType.DMA((copies,))] * 2
         + [pltpu.SemaphoreType.DMA((n + 1,))] * 2,
-        compiler_params=pltpu.CompilerParams(collective_id=2, has_side_effects=True, vmem_limit_bytes=32 << 20),
+        compiler_params=pltpu.CompilerParams(collective_id=2, has_side_effects=True, vmem_limit_bytes=60 << 20),
         name="final_exchange",
     )(rows, *halves)
 
@@ -379,9 +381,14 @@
         name="window_attention")(q, k, v, ones)
 
 
-def dec_kernel(idx, cnt, x, wk, wv, gs, wq, wo, out, table, q3, prod, sc, mix3, seg):
+def dec_kernel(idx, x, wk, wv, cnt, gs, wq, wo, out, table, q3, prod_a, held_a, prod_b, held_b, mix3, seg, live):
     i = pl.program_id(0)
-    tsteps = table.shape[0] // RB
+    tsteps = table.shape[0] // (2 * RB)
+    rows = table.shape[0] // 2
+    lines = table.reshape(table.shape[0] * 8, 128)
+    qlines = q3.reshape(GB * 8, 128)
+    lives = live.reshape(E_DEC * GB, 128)
+    mlines = mix3.reshape(GB * 8, 128)
     lane = lax.broadcasted_iota(jnp.int32, (1, 128), 1)
 
     @pl.when(i == 0)
@@ -396,40 +403,66 @@
         cen = xf - jnp.mean(xf, axis=-1, keepdims=True)
         var = jnp.mean(cen * cen, axis=-1, keepdims=True)
         xn = (cen * lax.rsqrt(var + EPSILON)).astype(jnp.bfloat16)
-        r0 = pl.multiple_of(i * RB, RB)
         for part, w in enumerate((wk, wk, wv, wv)):
-            kv = jnp.dot(xn, w[:, (part % 2) * 512:(part % 2 + 1) * 512], preferred_element_type=jnp.float32)
+            kv = jnp.dot(xn, w[:, part % 2 * 512:part % 2 * 512 + 512], preferred_element_type=jnp.float32)
             for s in range(4):
-                table[pl.ds(r0, RB), part * 4 + s, :] = kv[:, s * 128:(s + 1) * 128]
+                lines[pl.ds(i * (RB * 8) + (part // 2 * rows * 8 + part % 2 * 4 + s), RB, stride=8), :] = kv[:, s * 128:(s + 1) * 128]
 
     @pl.when(i >= tsteps)
     def _():
         b = i - tsteps
         g0 = b * GB
         gb = gs[...]
-        qf = jnp.dot(gb, wq[...], preferred_element_type=jnp.float32) * SCALE
+        qf = jnp.dot(gb, wq[...], preferred_element_type=jnp.float32) * (SCALE * LOG2E)
         for s in range(8):
-            q3[:, s, :] = qf[:, s * 128:(s + 1) * 128]
-        for g in range(GB):
-            qv = q3[g]
-            for e in range(E_DEC):
-                prod[e, g] = qv * table[idx[(g0 + g) * E_DEC + e], 0:8, :]
-        pm = prod[...].reshape(E_DEC * GB * 8, 128).astype(jnp.bfloat16)
-        sc[...] = jnp.exp(jnp.dot(pm, seg[...], preferred_element_type=jnp.float32)).reshape(E_DEC, GB, 8, 128)
-        for g in range(GB):
-            c = cnt[g0 + g]
-            tot = None
-            acc = None
-            for e in range(E_DEC):
-                pe = sc[e, g]
-                if e > 0:
-                    pe = jnp.where(e < c, pe, 0.0)
-                pv = pe * table[idx[(g0 + g) * E_DEC + e], 8:16, :]
-                tot = pe if e == 0 else tot + pe
-                acc = pv if e == 0 else acc + pv
-            mix3[g] = acc / tot
+            q3[:, s] = qf[:, s * 128:(s + 1) * 128].reshape(GB // 8, 8, 128)
+        for e in range(E_DEC):
+            live[e] = jnp.broadcast_to(jnp.where(cnt[...] > e, 1.0, 0.0), (GB, 128))
+
+        def gather(o, prod, held):
+            base = (g0 + o * UN) * E_DEC
+            for j in range(UN):
+                place = (j // 8) * 64 + j % 8
+                qv = qlines[pl.ds(pl.multiple_of(o * (UN * 8), 64) + place, 8, stride=8), :]
+                parts = []
+                for e in range(E_DEC):
+                    at = pl.multiple_of(idx[base + (j * E_DEC + e)], 8)
+                    parts.append(qv * lines[pl.ds(at, 8), :])
+                    held[j, e] = lines[pl.ds(at + rows * 8, 8), :]
+                for h in range(E_DEC // 2):
+                    prod[j, h] = jnp.concatenate(parts[2 * h:2 * h + 2], axis=0).astype(jnp.bfloat16)
+
+        def mixing(o, prod, held):
+            pm = prod[...].reshape(E_DEC * UN * 8, 128)
+            sc = jnp.dot(pm, seg[...], preferred_element_type=jnp.float32).reshape(UN, E_DEC, 8, 128)
+            for j in range(UN):
+                tot = None
+                for e in range(E_DEC):
+                    pe = jnp.exp2(sc[j, e])
+                    if e > 0:
+                        pe = pe * lives[pl.ds(e * GB + (o * UN + j), 8, stride=0), :]
+                    pv = pe * held[j, e]
+                    tot = pe if e == 0 else tot + pe
+                    acc = pv if e == 0 else acc + pv
+                place = (j // 8) * 64 + j % 8
+                mlines[pl.ds(pl.multiple_of(o * (UN * 8), 64) + place, 8, stride=8), :] = acc / tot
+
+        rounds = GB // UN
+        gather(0, prod_a, held_a)
+
+        def both(o, carry):
+            gather(2 * o + 1, prod_b, held_b)
+            mixing(2 * o, prod_a, held_a)
+            gather(2 * o + 2, prod_a, held_a)
+            mixing(2 * o + 1, prod_b, held_b)
+            return carry
+
+        lax.fori_loop(0, rounds // 2 - 1, both, 0)
+        gather(rounds - 1, prod_b, held_b)
+        mixing(rounds - 2, prod_a, held_a)
+        mixing(rounds - 1, prod_b, held_b)
         o = gb.astype(jnp.float32)
-        m2 = jnp.concatenate([mix3[:, s, :] for s in range(8)], axis=1).astype(jnp.bfloat16)
+        m2 = jnp.concatenate([mix3[:, s].reshape(GB, 128) for s in range(8)], axis=1).astype(jnp.bfloat16)
         o = o + jnp.dot(m2, wo[...], preferred_element_type=jnp.float32)
         out[...] = o[:, :out.shape[1]].astype(jnp.bfloat16)
 
@@ -444,21 +477,24 @@
         dec_kernel,
         out_shape=jax.ShapeDtypeStruct((grid_rows, variables), jnp.bfloat16),
         grid_spec=pltpu.PrefetchScalarGridSpec(
-            num_scalar_prefetch=2, grid=(steps,),
+            num_scalar_prefetch=1, grid=(steps,),
             in_specs=[pl.BlockSpec((RB, width), lambda i, *_: (jnp.minimum(i, tsteps - 1), 0)),
                       full(wk), full(wv),
-                      pl.BlockSpec((GB, 128), late), full(wq), full(wo)],
+                      pl.BlockSpec((GB, 1), late), pl.BlockSpec((GB, 128), late), full(wq), full(wo)],
             out_specs=pl.BlockSpec((GB, variables), late),
             scratch_shapes=[
-                pltpu.VMEM((rows, 16, 128), jnp.float32),
-                pltpu.VMEM((GB, 8, 128), jnp.float32),
-                pltpu.VMEM((E_DEC, GB, 8, 128), jnp.float32),
-                pltpu.VMEM((E_DEC, GB, 8, 128), jnp.float32),
-                pltpu.VMEM((GB, 8, 128), jnp.float32),
-                pltpu.VMEM((128, 128), jnp.bfloat16)]),
+                pltpu.VMEM((2 * rows, 8, 128), jnp.float32),
+                pltpu.VMEM((GB // 8, 8, 8, 128), jnp.float32),
+                pltpu.VMEM((UN, E_DEC // 2, 16, 128), jnp.bfloat16),
+                pltpu.VMEM((UN, E_DEC, 8, 128), jnp.float32),
+                pltpu.VMEM((UN, E_DEC // 2, 16, 128), jnp.bfloat16),
+                pltpu.VMEM((UN, E_DEC, 8, 128), jnp.float32),
+                pltpu.VMEM((GB // 8, 8, 8, 128), jnp.float32),
+                pltpu.VMEM((128, 128), jnp.bfloat16),
+                pltpu.VMEM((E_DEC, GB, 128), jnp.float32)]),
         compiler_params=pltpu.CompilerParams(dimension_semantics=("arbitrary",), vmem_limit_bytes=56 << 20),
         name="dec_attention",
-    )(sources.reshape(-1), counts, x, wk, wv, gs, wq, wo)
+    )((sources * 8).reshape(-1), x, wk, wv, counts[:, None], gs, wq, wo)
 
 
 def local(

time: 287 us -> 252 us (0.88)
  Pallas kernels: 216 us -> 188 us
  local copies, waits for them, and re-layouts: 34 us -> 19.4 us
  matrix products: 32.4 us -> 36 us
  other arithmetic: 2.64 us -> 6.11 us
    pallas_call x1, Pallas kernels: 85.2 us -> 54.8 us  [decode(): pl.pallas_call(dec_kernel, out_shape=jax.ShapeDtypeStruct((grid_rows, var...]
    unnamed x63 -> x49, local copies, waits for them, and re-layouts: 20.6 us -> 5.96 us
    dot_general x4, matrix products: 12.5 us -> 17.6 us  [project(): jnp.dot(matrix, weight, preferred_element_type=jnp.float32)]
    dynamic_slice x5 -> x6, local copies, waits for them, and re-layouts: 4.36 us -> 1.11 us  [local(): my_rows = lambda a, size: lax.dynamic_slice_in_dim(a, head * size, size, 0)]
where the time goes in v2:
time: 252 us; the launch traced here: 251 us
  Pallas kernels  188 us (75%)
  matrix products  36 us (14%)
  local copies, waits for them, and re-layouts  19.4 us (8%)
  other arithmetic  6.11 us (2%)
    pallas_call x1, Pallas kernels, decode(): pl.pallas_call(dec_kernel, out_shape=jax.ShapeDtypeStruct((grid_rows, var...  54.8 us
    pallas_call x1, Pallas kernels, enc_attention(): pl.pallas_call(enc_kernel, out_shape=jax.ShapeDtypeStruct((nodes, width),...  34.7 us
    pallas_call x1, Pallas kernels, final_exchange(): pl.pallas_call(functools.partial(final_kernel_exchange, n, dims), out_sha...  34.6 us
    pallas_call x1, Pallas kernels, start_exchange(): pl.pallas_call(functools.partial(start_kernel, n, dims), out_shape=outs,...  26.2 us
    pallas_call x1, Pallas kernels, window_exchange(): pl.pallas_call(functools.partial(window_kernel_exchange, n, dims), out_sh...  22.7 us
    dot_general x4, matrix products, project(): jnp.dot(matrix, weight, preferred_element_type=jnp.float32)  17.6 us
    dot_general x1, matrix products, local(): jnp.dot(inner, down, preferred_element_type=jnp.float32)  15.8 us
    pallas_call x1, Pallas kernels, window(): pl.pallas_call(win_kernel, out_shape=jax.ShapeDtypeStruct((nodes, width),...  15.5 us

profile of v2, /device:TPU:1, one launch (start us, length us, event | category | flops | bytes accessed | tf_op | source)
XLA Modules:
  0.0 251.0 jit_solution(7751147752224585517)
XLA Ops:
  0.7 0.9 subtract_multiply_fusion
  1.9 1.2 reshape.100.idx
  3.5 0.7 copy.26
  4.2 1.3 pad.18.refs_0_.go
  5.5 0.7 pad.19.refs_2_
  6.1 0.7 pad.20.refs_3_
  7.6 0.7 pad.22.refs_11_
  8.3 26.2 %start_exchange.1 = (bf16[8192,128]{1,0:T(8,128)(2,1)}, bf16[512,1024]{1,0:T(8,128)(2,1)}, bf16[128,1024]{1,0:T(8,128)(2,1)}, bf16[128,1024]{1,0:T(8,128)(2,1)},...) custom-call(bf16[4096,128]{1,0:T(8,128)(2,1)} %pad.18.refs_0_.go, ...), custom_call_target="tpu_custom_call" | custom-call | tf_op jit(solution)/shard_map/start_exchange/pallas_call | solution.py:140
  34.5 1.5 convert_reduce_fusion.2
  36.0 1.6 fusion.20
  37.7 4.0 %convolution_convert_fusion.3.q = bf16[512,1024]{1,0:T(8,128)(2,1)} fusion(bf16[1024,1024]{1,0:T(8,128)(2,1)} %get-tuple-element.21, bf16[512,1024]{1,0:T(8,128)(2,1)S(1)} %copy-done.10, f32[512]{0:T(512)S(1)} %add_rsqrt_fusion.2, f32[512]{0:T(512)S(1)} %broadcast_multiply_fusion.2), kind=kOutput, calls=%fused_computation.38 | convolution fusion | flops 1076363264 | bytes 4198400 | tf_op jit(solution)/shard_map/dot_general | solution.py:34
  41.9 0.8 lt.64
  42.7 1.7 lt.65
  44.5 0.9 compare_select_fusion.bias
  45.5 0.9 copy-done.5
  46.4 1.2 copy-done.6
  47.6 34.7 %enc_attention.1 = bf16[512,1024]{1,0:T(8,128)(2,1)S(1)} custom-call(s32[16384]{0:T(1024)S(1)} %reshape.101.idx, bf16[512,1024]{1,0:T(8,128)(2,1)S(1)} %copy-done.6, bf16[128,1024]{1,0:T(8,128)(2,1)S(1)} %copy-done.4, bf16[128,1024]{1,0:T(8,128)(2,1)S(1)} %copy-done.5, bf16[4096,128]{1,0:T(8,128)(2,1)S(1)} %copy-done.2, bf16[8192,128]{1,0:T(8,128)(2,1)S(1)} %copy-done.3, ...), custom_call_target="tpu_custom_call" | custom-call | flops 4294967296 | bytes 8388608 | tf_op jit(solution)/shard_map/enc_attention/pallas_call | solution.py:325
  82.3 1.3 convert_reduce_fusion.1
  84.4 0.8 copy-done.21
  85.3 1.3 convolution_convert_fusion.2.q
  86.5 22.7 %window_exchange.1 = (bf16[1664,1024]{1,0:T(8,128)(2,1)}, bf16[1024,4096]{1,0:T(8,128)(2,1)}, bf16[4096,1024]{1,0:T(8,128)(2,1)}) custom-call(bf16[512,1024]{1,0:T(8,128)(2,1)} %copy-done.9, bf16[1024,2048]{1,0:T(8,128)(2,1)} %refs_1_.4, bf16[2048,1024]{1,0:T(8,128)(2,1)} %refs_2_.2), custom_call_target="tpu_custom_call" | custom-call | tf_op jit(solution)/shard_map/window_exchange/pallas_call | solution.py:198
  109.3 6.5 %convolution_convert_fusion.1.k = bf16[1664,1024]{1,0:T(8,128)(2,1)S(1)} fusion(bf16[1024,1024]{1,0:T(8,128)(2,1)} %get-tuple-element.28, bf16[1664,1024]{1,0:T(8,128)(2,1)} %get-tuple-element.27, pred[1664]{0:T(1024)(128)(4,1)S(1)} %get-tuple-element.46), kind=kOutput, calls=%fused_computation.11 | convolution fusion | flops 3493068800 | bytes 8914560 | tf_op jit(solution)/shard_map/dot_general | solution.py:34
  115.9 5.7 %convolution_convert_fusion.v = bf16[1664,1024]{1,0:T(8,128)(2,1)} fusion(bf16[1024,1024]{1,0:T(8,128)(2,1)S(1)} %copy-done.20, bf16[1664,1024]{1,0:T(8,128)(2,1)S(1)} %copy-done.18, pred[1664]{0:T(1024)(128)(4,1)S(1)} %get-tuple-element.46), kind=kOutput, calls=%fused_computation.10 | convolution fusion | flops 3493068800 | bytes 8914560 | tf_op jit(solution)/shard_map/dot_general | solution.py:34
  121.9 15.5 %window_attention.1 = bf16[512,1024]{1,0:T(8,128)(2,1)S(1)} custom-call(bf16[512,1024]{1,0:T(8,128)(2,1)S(1)} %convolution_convert_fusion.2.q, bf16[1664,1024]{1,0:T(8,128)(2,1)S(1)} %convolution_convert_fusion.1.k, bf16[1664,1024]{1,0:T(8,128)(2,1)} %convolution_convert_fusion.v, bf16[1664,128]{1,0:T(8,128)(2,1)S(1)} %broadcast_in_dim.40.ones), custom_call_target="tpu_custom_call" | custom-call | tf_op jit(solution)/shard_map/window_attention/pallas_call | solution.py:373
  137.5 1.3 convert_reduce_fusion
  139.3 15.8 %fusion.24.refs_0_ = bf16[512,1024]{1,0:T(8,128)(2,1)} fusion(bf16[512,1024]{1,0:T(8,128)(2,1)S(1)} %get-tuple-element.45, bf16[4096,1024]{1,0:T(8,128)(2,1)} %get-tuple-element.32, bf16[1024,4096]{1,0:T(8,128)(2,1)} %get-tuple-element.31, f32[512]{0:T(512)S(1)} %add_rsqrt_fusion, f32[512]{0:T(512)S(1)} %broadcast_multiply_fusion), kind=kOutput, calls=%fused_computation.36 | convolution fusion | flops 8612478976 | bytes 18878464 | tf_op jit(solution)/shard_map/dot_general | solution.py:555
  155.1 34.6 %final_exchange.1 = (bf16[3072,1024]{1,0:T(8,128)(2,1)}, bf16[1024,1024]{1,0:T(8,128)(2,1)}, bf16[1024,1024]{1,0:T(8,128)(2,1)}) custom-call(bf16[512,1024]{1,0:T(8,128)(2,1)} %fusion.24.refs_0_, bf16[1024,512]{1,0:T(8,128)(2,1)} %refs_1_.5, bf16[1024,512]{1,0:T(8,128)(2,1)} %refs_2_.3), custom_call_target="tpu_custom_call" | custom-call | tf_op jit(solution)/shard_map/final_exchange/pallas_call | solution.py:254
  189.6 1.3 copy.29.cnt
  191.0 0.9 constant_dynamic-slice_fusion.gs
  191.9 54.8 %dec_attention.1 = bf16[2048,100]{1,0:T(8,128)(2,1)} custom-call(s32[8192]{0:T(1024)} %reshape.100.idx, bf16[3072,1024]{1,0:T(8,128)(2,1)} %get-tuple-element.33.x, bf16[1024,1024]{1,0:T(8,128)(2,1)} %get-tuple-element.34.wk, bf16[1024,1024]{1,0:T(8,128)(2,1)} %get-tuple-element.35.wv, s32[2048,1]{1,0:T(8,128)} %copy.29.cnt, ...), custom_call_target="tpu_custom_call" | custom-call | tf_op jit(solution)/shard_map/dec_attention/pallas_call | solution.py:476
  246.7 2.1 copy.30
  248.7 2.3 constant_dynamic-slice_fusion.2
  (66 shorter events, 3.2 us)
Async XLA Ops:
  0.6 2.5 copy-start
  0.6 2.8 %copy-start.12 = (bf16[4096,100]{0,1:T(8,128)(2,1)S(1)}, bf16[4096,100]{0,1:T(8,128)(2,1)}, u32[]{:S(2)}) copy-start(bf16[4096,100]{0,1:T(8,128)(2,1)} %param.20) | copy-start | bytes 2457604
  3.3 2.2 copy-start.13
  3.4 2.7 %copy-start.14 = (bf16[100,512]{1,0:T(8,128)(2,1)S(1)}, bf16[100,512]{1,0:T(8,128)(2,1)}, u32[]{:S(2)}) copy-start(bf16[100,512]{1,0:T(8,128)(2,1)} %param.27) | copy-start | bytes 307204
  3.4 3.4 %copy-start.15 = (bf16[100,512]{1,0:T(8,128)(2,1)S(1)}, bf16[100,512]{1,0:T(8,128)(2,1)}, u32[]{:S(2)}) copy-start(bf16[100,512]{1,0:T(8,128)(2,1)} %param.36) | copy-start | bytes 307204
  3.4 4.0 %copy-start.16 = (bf16[512,100]{0,1:T(8,128)(2,1)S(1)}, bf16[512,100]{0,1:T(8,128)(2,1)}, u32[]{:S(2)}) copy-start(bf16[512,100]{0,1:T(8,128)(2,1)} %param.39) | copy-start | bytes 307204
  4.1 30.3 %copy-start.7 = (bf16[4096,100]{1,0:T(8,128)(2,1)}, bf16[4096,100]{1,0:T(8,128)(2,1)S(1)}, u32[]{:S(2)}) copy-start(bf16[4096,100]{1,0:T(8,128)(2,1)S(1)} %copy.26) | copy-start | bytes 2457604
  34.4 3.2 %copy-start.10 = (bf16[512,1024]{1,0:T(8,128)(2,1)S(1)}, bf16[512,1024]{1,0:T(8,128)(2,1)}, u32[]{:S(2)}) copy-start(bf16[512,1024]{1,0:T(8,128)(2,1)} %get-tuple-element.20) | copy-start | bytes 3145732
  37.6 4.1 %copy-start.17 = (s32[1024]{0:T(1024)S(1)}, s32[1024]{0:T(1024)}, u32[]{:S(2)}) copy-start(s32[1024]{0:T(1024)} %param.23) | copy-start | bytes 12292
  37.7 7.8 %copy-start.2 = (bf16[4096,128]{1,0:T(8,128)(2,1)S(1)}, bf16[4096,128]{1,0:T(8,128)(2,1)}, u32[]{:S(2)}) copy-start(bf16[4096,128]{1,0:T(8,128)(2,1)} %pad.18.refs_0_.go) | copy-start | bytes 3145732
  37.7 7.8 %copy-start.3 = (bf16[8192,128]{1,0:T(8,128)(2,1)S(1)}, bf16[8192,128]{1,0:T(8,128)(2,1)}, u32[]{:S(2)}) copy-start(bf16[8192,128]{1,0:T(8,128)(2,1)} %get-tuple-element.24.near) | copy-start | bytes 6291460
  37.7 7.8 %copy-start.4 = (bf16[128,1024]{1,0:T(8,128)(2,1)S(1)}, bf16[128,1024]{1,0:T(8,128)(2,1)}, u32[]{:S(2)}) copy-start(bf16[128,1024]{1,0:T(8,128)(2,1)} %get-tuple-element.22.wk) | copy-start | bytes 786436
  45.5 1.0 copy-start.5
  46.4 1.2 copy-start.6
  47.6 34.7 %copy-start.11 = (bf16[512,1024]{1,0:T(8,128)(2,1)S(1)}, bf16[512,1024]{1,0:T(8,128)(2,1)}, u32[]{:S(2)}) copy-start(bf16[512,1024]{1,0:T(8,128)(2,1)} %get-tuple-element.20) | copy-start | bytes 3145732
  47.6 34.7 %copy-start.22 = (bf16[1024,1024]{1,0:T(8,128)(2,1)S(1)}, bf16[1024,1024]{1,0:T(8,128)(2,1)}, u32[]{:S(2)}) copy-start(bf16[1024,1024]{1,0:T(8,128)(2,1)} %get-tuple-element.25) | copy-start | bytes 6291460
  83.7 1.6 copy-start.21
  84.4 2.1 copy-start.9
  109.3 6.6 %copy-start.18 = (bf16[1664,1024]{1,0:T(8,128)(2,1)S(1)}, bf16[1664,1024]{1,0:T(8,128)(2,1)}, u32[]{:S(2)}) copy-start(bf16[1664,1024]{1,0:T(8,128)(2,1)} %get-tuple-element.27) | copy-start | bytes 10223620
  109.3 6.6 %copy-start.20 = (bf16[1024,1024]{1,0:T(8,128)(2,1)S(1)}, bf16[1024,1024]{1,0:T(8,128)(2,1)}, u32[]{:S(2)}) copy-start(bf16[1024,1024]{1,0:T(8,128)(2,1)} %get-tuple-element.29) | copy-start | bytes 6291460
  121.9 15.6 %copy-start.19 = (bf16[1024,1024]{1,0:T(8,128)(2,1)S(1)}, bf16[1024,1024]{1,0:T(8,128)(2,1)}, u32[]{:S(2)}) copy-start(bf16[1024,1024]{1,0:T(8,128)(2,1)} %get-tuple-element.30) | copy-start | bytes 6291460
  155.1 34.6 %dynamic-slice-start = ((s32[4096]{0:T(1024)}, s32[]{:T(128)}), s32[2048]{0:T(1024)S(1)}, s32[]{:S(2)}) async-start(s32[4096]{0:T(1024)} %param.25, s32[]{:T(128)} %select_n.25), calls=%async_computation | async-start | bytes 16896 | tf_op jit(solution)/shard_map/dynamic_slice | solution.py:537
  155.1 35.9 %copy-start.8 = (bf16[4096,100]{1,0:T(8,128)(2,1)S(1)}, bf16[4096,100]{1,0:T(8,128)(2,1)}, u32[]{:S(2)}) copy-start(bf16[4096,100]{1,0:T(8,128)(2,1)} %copy-done.7) | copy-start | bytes 2457604
  191.9 59.1 %copy-start.1 = (s32[1024,32]{0,1:T(8,128)S(1)}, s32[1024,32]{0,1:T(8,128)}, u32[]{:S(2)}) copy-start(s32[1024,32]{0,1:T(8,128)} %param.22) | copy-start | bytes 393220

commit v3 on v2

--- a/solution.py
+++ b/solution.py
@@ -18,7 +18,6 @@
 QB = 128
 GB = 128
 UN = 16
-RB = 256
 ANY = pl.BlockSpec(memory_space=pltpu.HBM)
 VM = pl.BlockSpec(memory_space=pltpu.VMEM)
 
@@ -151,117 +150,220 @@
     )(grid, state, *halves)
 
 
-def window_kernel_exchange(n_pair, dims, *refs):
-    rows = refs[0]
-    halves = refs[1 : 1 + n_pair]
-    span = refs[1 + n_pair]
-    fulls = refs[2 + n_pair : 2 + 2 * n_pair]
-    rest = refs[2 + 2 * n_pair :]
-    holds = rest[:n_pair]
-    send_sem, recv_sem, load_sem, store_sem = rest[n_pair:]
+def span_kernel(n_pair, dims, *refs):
+    rows, wq, wk, wv = refs[:4]
+    halves = refs[4 : 4 + n_pair]
+    q, k, v = refs[4 + n_pair : 7 + n_pair]
+    fulls = refs[7 + n_pair : 7 + 2 * n_pair]
+    span, hold_q, hold_k, hold_v = refs[7 + 2 * n_pair : 11 + 2 * n_pair]
+    holds = refs[11 + 2 * n_pair : 11 + 3 * n_pair]
+    send_sem, recv_sem, load_sem, store_sem = refs[11 + 3 * n_pair :]
     band, head, left, right = places()
-    count = rows.shape[0]
+    bands = lax.axis_size("band")
+    count, width = rows.shape
     extra = HALF_WIN - count
     after = HALF_WIN + count
+    chunks = 4
+    step = count // chunks
     peer = (band, 1 - head)
-    across = (lax.rem(band + lax.axis_size("band") + 2 * head - 1, lax.axis_size("band")), 1 - head)
-    loads = [pltpu.make_async_copy(h, v, load_sem.at[n]) for n, (h, v) in enumerate(zip(halves, holds))]
+    beside = (lax.rem(band + bands + 2 * head - 1, bands), 1 - head)
+    weights = [pltpu.make_async_copy(w, hold, load_sem.at[n_pair + n]) for n, (w, hold) in enumerate(((wq, hold_q), (wk, hold_k), (wv, hold_v)))]
+    for load in weights:
+        load.start()
+    loads = [pltpu.make_async_copy(h, hold, load_sem.at[n]) for n, (h, hold) in enumerate(zip(halves, holds))]
     for load in loads:
         load.start()
-    own = pltpu.make_async_copy(rows, span.at[pl.ds(HALF_WIN, count)], store_sem.at[n_pair])
-    own.start()
-    greet([peer, (left, head), (right, head), across])
+    greet([peer, (left, head), (right, head), beside])
     sender = Sender(send_sem, recv_sem)
-    sender.send(rows, span.at[pl.ds(pl.multiple_of(after + head * (extra - after), 16), count)], across)
-    sender.send(rows.at[pl.ds(count - extra, extra)], span.at[pl.ds(0, extra)], (right, head))
-    sender.send(rows.at[pl.ds(0, extra)], span.at[pl.ds(after + count, extra)], (left, head))
-    sender.send(rows, span.at[pl.ds(pl.multiple_of(extra + head * (after - extra), 16), count)], peer)
+    from_beside = extra + head * (after - extra)
+    from_peer = after + head * (extra - after)
+    first = sender.send(rows.at[pl.ds(count - extra, extra)], span.at[pl.ds(0, extra)], (right, head))
+    last = sender.send(rows.at[pl.ds(0, extra)], span.at[pl.ds(after + count, extra)], (left, head))
+    waves = [sender.send(rows.at[pl.ds(c * step, step)], span.at[pl.ds(pl.multiple_of(from_peer + c * step, 16), step)], beside)
+             for c in range(chunks)]
+    partner = sender.send(rows, span.at[pl.ds(pl.multiple_of(from_beside, 16), count)], peer)
     for n in range(n_pair):
         sender.send(halves[n], half_of(fulls[n], dims[n], head), peer)
+    for load in weights:
+        load.wait()
+
+    def pair(x, place, size):
+        node = band * (2 * count) + head * count - HALF_WIN + place + lax.broadcasted_iota(jnp.int32, (size, 1), 0)
+        live = (node >= 0) & (node < bands * 2 * count)
+        for w, o in ((hold_k, k), (hold_v, v)):
+            o[pl.ds(place, size), :] = jnp.where(live, jnp.dot(x, w[...], preferred_element_type=jnp.float32), 0.0).astype(jnp.bfloat16)
+
+    half = count // 2
+    for b in range(2):
+        x = rows[b * half:(b + 1) * half, :]
+        q[b * half:(b + 1) * half, :] = jnp.dot(x, hold_q[...], preferred_element_type=jnp.float32).astype(jnp.bfloat16)
+        pair(x, HALF_WIN + b * half, half)
     stores = [pltpu.make_async_copy(holds[n], half_of(fulls[n], dims[n], head), store_sem.at[n]) for n in range(n_pair)]
     for load, store in zip(loads, stores):
         load.wait()
         store.start()
-    sender.finish()
-    own.wait()
+    partner.wait_recv()
+    for b in range(2):
+        place = pl.multiple_of(from_peer + b * half, 16)
+        pair(span[pl.ds(place, half), :], place, half)
+    first.wait_recv()
+    last.wait_recv()
+    tail = span.shape[0] - after - count - extra
+    pad = jnp.zeros((tail, width), rows.dtype)
+    pair(span[0:extra, :], 0, extra)
+    pair(jnp.concatenate((span[after + count:after + count + extra, :], pad), axis=0), after + count, extra + tail)
+    for b in range(2):
+        for c in range(b * chunks // 2, (b + 1) * chunks // 2):
+            waves[c].wait_recv()
+        place = pl.multiple_of(from_beside + b * half, 16)
+        pair(span[pl.ds(place, half), :], place, half)
+    sender.finish(waves + [first, last, partner])
     for store in stores:
         store.wait()
 
 
-def window_exchange(rows, span_rows, pairs):
+def window_span(rows, span_rows, wq, wk, wv, pairs):
     halves = [half for half, _ in pairs]
     dims = [dim for _, dim in pairs]
     n = len(pairs)
-    outs = [jax.ShapeDtypeStruct((span_rows, rows.shape[1]), rows.dtype)]
+    outs = [jax.ShapeDtypeStruct((size, rows.shape[1]), rows.dtype) for size in (rows.shape[0], span_rows, span_rows)]
     outs += [full_shape(half, dim) for half, dim in pairs]
-    copies = 4 + n
+    copies = 7 + n
     return pl.pallas_call(
-        functools.partial(window_kernel_exchange, n, dims),
+        functools.partial(span_kernel, n, dims),
         out_shape=outs,
-        in_specs=[VM] + [ANY] * n,
-        out_specs=[ANY] * (n + 1),
-        scratch_shapes=[pltpu.VMEM(half.shape, half.dtype) for half in halves]
+        in_specs=[VM] + [ANY] * (n + 3),
+        out_specs=[VM] * 3 + [ANY] * n,
+        scratch_shapes=[pltpu.VMEM((span_rows, rows.shape[1]), rows.dtype)]
+        + [pltpu.VMEM(w.shape, w.dtype) for w in (wq, wk, wv)]
+        + [pltpu.VMEM(half.shape, half.dtype) for half in halves]
         + [pltpu.SemaphoreType.DMA((copies,))] * 2
-        + [pltpu.SemaphoreType.DMA((n + 1,))] * 2,
-        compiler_params=pltpu.CompilerParams(collective_id=1, has_side_effects=True, vmem_limit_bytes=60 << 20),
-        name="window_exchange",
-    )(rows, *halves)
-
-
-def final_kernel_exchange(n_pair, dims, *refs):
-    rows = refs[0]
-    halves = refs[1 : 1 + n_pair]
-    near = refs[1 + n_pair]
-    fulls = refs[2 + n_pair : 2 + 2 * n_pair]
-    rest = refs[2 + 2 * n_pair :]
-    holds = rest[:n_pair]
-    send_sem, recv_sem, load_sem, store_sem = rest[n_pair:]
+        + [pltpu.SemaphoreType.DMA((n + 3,)), pltpu.SemaphoreType.DMA((n,))],
+        compiler_params=pltpu.CompilerParams(collective_id=1, has_side_effects=True, vmem_limit_bytes=46 << 20),
+        name="window_span",
+    )(rows, wq, wk, wv, *halves)
+
+
+def tables_kernel(rows, wk, wv, table, out, near, hold_k, hold_v, blocks, send_sem, recv_sem, load_sem, store_sem):
     band, head, left, right = places()
-    count = rows.shape[0]
+    count, width = rows.shape
+    chunks = 4
+    step = count // chunks
     peer = (band, 1 - head)
-    loads = [pltpu.make_async_copy(h, v, load_sem.at[n]) for n, (h, v) in enumerate(zip(halves, holds))]
+    lines = blocks.reshape(blocks.shape[0] * blocks.shape[1] * blocks.shape[2] * 8, 128)
+    loads = [pltpu.make_async_copy(half, half_of(hold, 1, head), load_sem.at[n])
+             for n, (half, hold) in enumerate(((wk, hold_k), (wv, hold_v)))]
     for load in loads:
         load.start()
+    greet([peer, (left, head), (right, head)])
+
+    def side_rows(side, c):
+        return pl.ds(pl.multiple_of(side * count + head * count + c * step, step), step)
+
+    def across(c, side):
+        return pltpu.make_async_remote_copy(
+            src_ref=rows.at[pl.ds(pl.multiple_of(c * step, step), step)], dst_ref=near.at[side_rows(side, c)],
+            send_sem=send_sem.at[2 * c + side // 4], recv_sem=recv_sem.at[2 * c + side // 4],
+            device_id=(left if side else right, head), device_id_type=MESH)
+
+    def passed(c, side):
+        ours = near.at[side_rows(side, c)]
+        n = 2 * c + side // 4 + 2 * chunks
+        return pltpu.make_async_remote_copy(
+            src_ref=ours, dst_ref=ours, send_sem=send_sem.at[n], recv_sem=recv_sem.at[n],
+            device_id=peer, device_id_type=MESH)
+
     mine = pl.ds(pl.multiple_of(2 * count + head * count, count), count)
-    own = pltpu.make_async_copy(rows, near.at[mine], store_sem.at[n_pair])
-    own.start()
-    greet([peer, (left, head), (right, head)])
-    sender = Sender(send_sem, recv_sem)
-    waves = relay(near, lambda o, c, step: rows.at[pl.ds(c * step, step)], 2 * count, (0, 2), sender, None, band, left, right, head, 4)
-    sender.send(rows, near.at[mine], peer)
-    for n in range(n_pair):
-        sender.send(halves[n], half_of(fulls[n], dims[n], head), peer)
-    stores = [pltpu.make_async_copy(holds[n], half_of(fulls[n], dims[n], head), store_sem.at[n]) for n in range(n_pair)]
-    for load, store in zip(loads, stores):
+    local = [pltpu.make_async_remote_copy(
+        src_ref=src, dst_ref=dst, send_sem=send_sem.at[4 * chunks + n], recv_sem=recv_sem.at[4 * chunks + n],
+        device_id=peer, device_id_type=MESH)
+        for n, (src, dst) in enumerate(((wk, half_of(hold_k, 1, head)), (wv, half_of(hold_v, 1, head)), (rows, near.at[mine])))]
+    for c in range(chunks):
+        for side in (0, 4):
+            across(c, side).start()
+    for copy in local:
+        copy.start()
+    near[mine, :] = rows[...]
+    for load in loads:
         load.wait()
-        store.start()
-    for copy, place in waves:
+    for copy in local:
         copy.wait_recv()
-        sender.send(near.at[place], near.at[place], peer)
-    sender.finish([copy for copy, _ in waves])
-    own.wait()
-    for store in stores:
-        store.wait()
-
-
-def final_exchange(rows, pairs):
-    halves = [half for half, _ in pairs]
-    dims = [dim for _, dim in pairs]
-    n = len(pairs)
-    outs = [jax.ShapeDtypeStruct((6 * rows.shape[0], rows.shape[1]), rows.dtype)]
-    outs += [full_shape(half, dim) for half, dim in pairs]
-    copies = 16 + 1 + n
+
+    def stores(base, slot):
+        return [pltpu.make_async_copy(
+            blocks.at[slot, kind, pl.ds(half * step, step)],
+            table.at[pl.ds(pl.multiple_of(kind * (6 * count) + base + half * count, step), step)],
+            store_sem.at[slot, 2 * kind + half]) for kind in range(2) for half in range(2)]
+
+    def project_block(base, turn):
+        slot = lax.rem(turn, 2)
+
+        @pl.when(turn >= 2)
+        def _():
+            for store in stores(base, slot):
+                store.wait()
+
+        pieces = [pl.multiple_of(base + part * count, step) for part in range(2)]
+        xf = jnp.concatenate([near[pl.ds(p, step), :] for p in pieces], axis=0).astype(jnp.float32)
+        cen = xf - jnp.mean(xf, axis=-1, keepdims=True)
+        var = jnp.mean(cen * cen, axis=-1, keepdims=True)
+        xn = (cen * lax.rsqrt(var + EPSILON)).astype(jnp.bfloat16)
+        for part, w in enumerate((hold_k, hold_k, hold_v, hold_v)):
+            kv = jnp.dot(xn, w[:, part % 2 * 512:part % 2 * 512 + 512], preferred_element_type=jnp.float32)
+            for s in range(4):
+                at = part // 2 * (2 * step * 8) + part % 2 * 4 + s
+                lines[pl.ds(slot * (4 * step * 8) + at, 2 * step, stride=8), :] = kv[:, s * 128:(s + 1) * 128]
+        for store in stores(base, slot):
+            store.start()
+
+    def own(c, carry):
+        project_block(2 * count + c * step, c)
+        return carry
+
+    lax.fori_loop(0, chunks, own, 0)
+    out[...] = near[2 * count:4 * count, pl.ds(pl.multiple_of(head * (width // 2), width // 2), width // 2)]
+
+    def waves(c, carry):
+        for side in (0, 4):
+            across(c, side).wait_recv()
+            passed(c, side).start()
+        for side in (0, 4):
+            passed(c, side).wait_recv()
+            project_block(side * count + c * step, chunks + 2 * c + side // 4)
+        return carry
+
+    lax.fori_loop(0, chunks, waves, 0)
+    for slot in range(2):
+        for store in stores(0, slot):
+            store.wait()
+    for c in range(chunks):
+        for side in (0, 4):
+            across(c, side).wait_send()
+            passed(c, side).wait_send()
+    for copy in local:
+        copy.wait_send()
+
+
+def final_tables(rows, wk, wv):
+    count, width = rows.shape
+    whole = (wk.shape[0], 2 * wk.shape[1])
     return pl.pallas_call(
-        functools.partial(final_kernel_exchange, n, dims),
-        out_shape=outs,
-        in_specs=[VM] + [ANY] * n,
-        out_specs=[ANY] * (n + 1),
-        scratch_shapes=[pltpu.VMEM(half.shape, half.dtype) for half in halves]
-        + [pltpu.SemaphoreType.DMA((copies,))] * 2
-        + [pltpu.SemaphoreType.DMA((n + 1,))] * 2,
+        tables_kernel,
+        out_shape=[jax.ShapeDtypeStruct((12 * count, 8, 128), jnp.float32), jax.ShapeDtypeStruct((2 * count, width // 2), rows.dtype)],
+        in_specs=[VM, ANY, ANY],
+        out_specs=[ANY, VM],
+        scratch_shapes=[
+            pltpu.VMEM((6 * count, width), rows.dtype),
+            pltpu.VMEM(whole, wk.dtype),
+            pltpu.VMEM(whole, wv.dtype),
+            pltpu.VMEM((2, 2, count // 2, 8, 128), jnp.float32),
+            pltpu.SemaphoreType.DMA((19,)),
+            pltpu.SemaphoreType.DMA((19,)),
+            pltpu.SemaphoreType.DMA((2,)),
+            pltpu.SemaphoreType.DMA((2, 4))],
         compiler_params=pltpu.CompilerParams(collective_id=2, has_side_effects=True, vmem_limit_bytes=60 << 20),
-        name="final_exchange",
-    )(rows, *halves)
+        name="final_tables",
+    )(rows, wk, wv)
 
 
 E_ENC = 32
@@ -381,9 +483,8 @@
         name="window_attention")(q, k, v, ones)
 
 
-def dec_kernel(idx, x, wk, wv, cnt, gs, wq, wo, out, table, q3, prod_a, held_a, prod_b, held_b, mix3, seg, live):
+def dec_kernel(idx, table, cnt, gs, wq, wo, out, q3, prod_a, held_a, prod_b, held_b, mix3, seg, live):
     i = pl.program_id(0)
-    tsteps = table.shape[0] // (2 * RB)
     rows = table.shape[0] // 2
     lines = table.reshape(table.shape[0] * 8, 128)
     qlines = q3.reshape(GB * 8, 128)
@@ -397,21 +498,8 @@
         c = lax.broadcasted_iota(jnp.int32, (128, 128), 1) // 64
         seg[...] = jnp.where(r == c, 1.0, 0.0).astype(jnp.bfloat16)
 
-    @pl.when(i < tsteps)
-    def _():
-        xf = x[...].astype(jnp.float32)
-        cen = xf - jnp.mean(xf, axis=-1, keepdims=True)
-        var = jnp.mean(cen * cen, axis=-1, keepdims=True)
-        xn = (cen * lax.rsqrt(var + EPSILON)).astype(jnp.bfloat16)
-        for part, w in enumerate((wk, wk, wv, wv)):
-            kv = jnp.dot(xn, w[:, part % 2 * 512:part % 2 * 512 + 512], preferred_element_type=jnp.float32)
-            for s in range(4):
-                lines[pl.ds(i * (RB * 8) + (part // 2 * rows * 8 + part % 2 * 4 + s), RB, stride=8), :] = kv[:, s * 128:(s + 1) * 128]
-
-    @pl.when(i >= tsteps)
-    def _():
-        b = i - tsteps
-        g0 = b * GB
+    def work():
+        g0 = i * GB
         gb = gs[...]
         qf = jnp.dot(gb, wq[...], preferred_element_type=jnp.float32) * (SCALE * LOG2E)
         for s in range(8):
@@ -466,24 +554,22 @@
         o = o + jnp.dot(m2, wo[...], preferred_element_type=jnp.float32)
         out[...] = o[:, :out.shape[1]].astype(jnp.bfloat16)
 
-def decode(x, wk, wv, gs, wq, wo, sources, counts, variables):
-    rows, width = x.shape
+    work()
+
+def decode(table, gs, wq, wo, sources, counts, variables):
     grid_rows = gs.shape[0]
-    tsteps = rows // RB
-    steps = tsteps + grid_rows // GB
+    steps = grid_rows // GB
     full = lambda a: pl.BlockSpec(a.shape, lambda i, *_: (0,) * a.ndim, pipeline_mode=pl.Buffered(1))
-    late = lambda i, *_: (jnp.maximum(i - tsteps, 0), 0)
+    late = lambda i, *_: (i, 0)
     return pl.pallas_call(
         dec_kernel,
         out_shape=jax.ShapeDtypeStruct((grid_rows, variables), jnp.bfloat16),
         grid_spec=pltpu.PrefetchScalarGridSpec(
             num_scalar_prefetch=1, grid=(steps,),
-            in_specs=[pl.BlockSpec((RB, width), lambda i, *_: (jnp.minimum(i, tsteps - 1), 0)),
-                      full(wk), full(wv),
+            in_specs=[full(table),
                       pl.BlockSpec((GB, 1), late), pl.BlockSpec((GB, 128), late), full(wq), full(wo)],
             out_specs=pl.BlockSpec((GB, variables), late),
             scratch_shapes=[
-                pltpu.VMEM((2 * rows, 8, 128), jnp.float32),
                 pltpu.VMEM((GB // 8, 8, 8, 128), jnp.float32),
                 pltpu.VMEM((UN, E_DEC // 2, 16, 128), jnp.bfloat16),
                 pltpu.VMEM((UN, E_DEC, 8, 128), jnp.float32),
@@ -492,9 +578,9 @@
                 pltpu.VMEM((GB // 8, 8, 8, 128), jnp.float32),
                 pltpu.VMEM((128, 128), jnp.bfloat16),
                 pltpu.VMEM((E_DEC, GB, 128), jnp.float32)]),
-        compiler_params=pltpu.CompilerParams(dimension_semantics=("arbitrary",), vmem_limit_bytes=56 << 20),
+        compiler_params=pltpu.CompilerParams(dimension_semantics=("arbitrary",), vmem_limit_bytes=60 << 20),
         name="dec_attention",
-    )((sources * 8).reshape(-1), x, wk, wv, counts[:, None], gs, wq, wo)
+    )((sources * 8).reshape(-1), table, counts[:, None], gs, wq, wo)
 
 
 def local(
@@ -541,22 +627,20 @@
     normed = layer_norm(mid)
     span = nodes + 2 * HALF_WIN
     span_rows = nodes - QB + -(-(QB + 2 * HALF_WIN) // 128) * 128
-    near, up, down = window_exchange(normed, span_rows, [(feed_up, 1), (feed_down, 0)])
+    query, keys, values, up, down = window_span(normed, span_rows, win_q, win_k, win_v, [(feed_up, 1), (feed_down, 0)])
     place = jnp.arange(span_rows, dtype=jnp.int32)
     node = band * band_nodes + head * nodes - HALF_WIN + place
     live = ((place < span) & (node >= 0) & (node < bands * band_nodes))[:, None]
-    near = jnp.where(live, near, jnp.zeros_like(near))
     ones = jnp.broadcast_to(live, (span_rows, 128)).astype(jnp.bfloat16)
-    mixed = window(project(normed, win_q), project(near, win_k), project(near, win_v), ones)
+    mixed = window(query, keys, values, ones)
     att = (mid.astype(jnp.float32) + jnp.dot(mixed, win_o, preferred_element_type=jnp.float32)).astype(jnp.bfloat16)
     inner = jax.nn.gelu(
         jnp.dot(layer_norm(att), up, preferred_element_type=jnp.float32), approximate=True
     ).astype(jnp.bfloat16)
     final = (att.astype(jnp.float32) + jnp.dot(inner, down, preferred_element_type=jnp.float32)).astype(jnp.bfloat16)
-    near_final, dec_k, dec_v = final_exchange(final, [(decoder_keys, 1), (decoder_values, 1)])
-    hidden_final = lax.dynamic_slice(near_final, (band_nodes, head * half_width), (band_nodes, half_width))
+    table, hidden_final = final_tables(final, decoder_keys, decoder_values)
     sources = my_rows(decoder_sources, half_grid) - (band - 1) * band_nodes
-    grid_next = decode(near_final, dec_k, dec_v, my_rows(grid, half_grid), dec_q, dec_o, sources,
+    grid_next = decode(table, my_rows(grid, half_grid), dec_q, dec_o, sources,
                        my_rows(decoder_counts, half_grid), variables)
     return (grid_next, hidden_final)
 

time: 252 us -> 233 us (0.925)
  matrix products: 36 us -> 22.6 us
  Pallas kernels: 188 us -> 182 us
  local copies, waits for them, and re-layouts: 19.4 us -> 22.1 us
    pallas_call x1, Pallas kernels: 54.8 us -> 39.4 us  [decode(): pl.pallas_call(dec_kernel, out_shape=jax.ShapeDtypeStruct((grid_rows, var...]
    dot_general x4 -> x1, matrix products: 17.6 us -> 4.07 us  [project(): jnp.dot(matrix, weight, preferred_element_type=jnp.float32)]
    pallas_call x2, Pallas kernels: 57.3 us -> 65.8 us  [the longest x1 41.5 us: final_tables(): pl.pallas_call(tables_kernel, out_shape=[jax.ShapeDtypeStruct((12 * count...]
    unnamed x49 -> x50, local copies, waits for them, and re-layouts: 5.96 us -> 10.9 us
where the time goes in v3:
time: 233 us
  Pallas kernels  182 us (78%)
  matrix products  22.6 us (10%)
  local copies, waits for them, and re-layouts  22.1 us (9%)
  other arithmetic  5.27 us (2%)
    pallas_call x1, Pallas kernels, final_tables(): pl.pallas_call(tables_kernel, out_shape=[jax.ShapeDtypeStruct((12 * count...  41.5 us
    pallas_call x1, Pallas kernels, decode(): pl.pallas_call(dec_kernel, out_shape=jax.ShapeDtypeStruct((grid_rows, var...  39.4 us
    pallas_call x1, Pallas kernels, enc_attention(): pl.pallas_call(enc_kernel, out_shape=jax.ShapeDtypeStruct((nodes, width),...  34.7 us
    pallas_call x1, Pallas kernels, start_exchange(): pl.pallas_call(functools.partial(start_kernel, n, dims), out_shape=outs,...  26.2 us
    pallas_call x1, Pallas kernels, window_span(): pl.pallas_call(functools.partial(span_kernel, n, dims), out_shape=outs, i...  24.3 us
    dot_general x1, matrix products, local(): jnp.dot(inner, down, preferred_element_type=jnp.float32)  15.8 us
    pallas_call x1, Pallas kernels, window(): pl.pallas_call(win_kernel, out_shape=jax.ShapeDtypeStruct((nodes, width),...  15.7 us
    unnamed x50, local copies, waits for them, and re-layouts  10.9 us

profile of v3, /device:TPU:1, one launch (start us, length us, event | category | flops | bytes accessed | tf_op | source)
XLA Modules:
  0.0 232.6 jit_solution(9131081674498226900)
XLA Ops:
  0.7 1.7 copy.26
  2.4 1.3 pad.18.refs_0_.go
  3.8 0.7 pad.22.refs_11_
  4.5 0.7 pad.19.refs_2_
  5.2 0.7 pad.20.refs_3_
  5.8 0.7 pad.21.refs_10_
  6.5 26.2 %start_exchange.1 = (bf16[8192,128]{1,0:T(8,128)(2,1)}, bf16[512,1024]{1,0:T(8,128)(2,1)}, bf16[128,1024]{1,0:T(8,128)(2,1)}, bf16[128,1024]{1,0:T(8,128)(2,1)},...) custom-call(bf16[4096,128]{1,0:T(8,128)(2,1)} %pad.18.refs_0_.go, ...), custom_call_target="tpu_custom_call" | custom-call | tf_op jit(solution)/shard_map/start_exchange/pallas_call | solution.py:139
  32.7 1.5 convert_reduce_fusion.2
  34.2 1.6 fusion.20
  35.9 4.1 %convolution_convert_fusion.q = bf16[512,1024]{1,0:T(8,128)(2,1)} fusion(bf16[1024,1024]{1,0:T(8,128)(2,1)} %get-tuple-element.22, bf16[512,1024]{1,0:T(8,128)(2,1)S(1)} %copy-done.12, f32[512]{0:T(512)S(1)} %add_rsqrt_fusion.2, f32[512]{0:T(512)S(1)} %broadcast_multiply_fusion.2), kind=kOutput, calls=%fused_computation.34 | convolution fusion | flops 1076363264 | bytes 4198400 | tf_op jit(solution)/shard_map/dot_general | solution.py:33
  40.3 0.8 lt.64
  41.2 0.9 compare_select_fusion.bias
  42.1 0.8 copy.28
  42.9 1.1 reshape.101.idx
  44.0 0.9 copy-done.7
  45.0 0.9 copy-done.8
  45.9 1.2 copy-done.9
  47.1 34.7 %enc_attention.1 = bf16[512,1024]{1,0:T(8,128)(2,1)S(1)} custom-call(s32[16384]{0:T(1024)S(1)} %reshape.101.idx, bf16[512,1024]{1,0:T(8,128)(2,1)S(1)} %copy-done.9, bf16[128,1024]{1,0:T(8,128)(2,1)S(1)} %copy-done.7, bf16[128,1024]{1,0:T(8,128)(2,1)S(1)} %copy-done.8, bf16[4096,128]{1,0:T(8,128)(2,1)S(1)} %copy-done.2, bf16[8192,128]{1,0:T(8,128)(2,1)S(1)} %copy-done.6, ...), custom_call_target="tpu_custom_call" | custom-call | flops 4294967296 | bytes 8388608 | tf_op jit(solution)/shard_map/enc_attention/pallas_call | solution.py:427
  81.9 1.3 convert_reduce_fusion.1
  84.0 0.9 copy-done.4
  84.9 24.3 %window_span.1 = (bf16[512,1024]{1,0:T(8,128)(2,1)S(1)}, bf16[1664,1024]{1,0:T(8,128)(2,1)}, bf16[1664,1024]{1,0:T(8,128)(2,1)}, bf16[1024,4096]{1,0:T(8,128)(2,1)}, bf16[4096,1024]{1,0:T(8,128)(2,1)}) custom-call(bf16[512,1024]{1,0:T(8,128)(2,1)S(1)} %fusion.19.refs_0_, bf16[1024,1024]{1,0:T(8,128)(2,1)S(1)} %copy-done.4, bf16[1024,1024]{1,0:T(8,128)(2,1)S(1)} %copy-done.5, ...), custom_call_target="tpu_custom_call" | custom-call | tf_op jit(solution)/shard_map/window_span/pallas_call | solution.py:232
  109.4 2.0 copy-done.3
  111.4 15.7 %window_attention.1 = bf16[512,1024]{1,0:T(8,128)(2,1)S(1)} custom-call(bf16[512,1024]{1,0:T(8,128)(2,1)S(1)} %get-tuple-element.30.q, bf16[1664,1024]{1,0:T(8,128)(2,1)S(1)} %copy-done.3, bf16[1664,1024]{1,0:T(8,128)(2,1)} %get-tuple-element.32.v, bf16[1664,128]{1,0:T(8,128)(2,1)S(1)} %broadcast_in_dim.14.ones), custom_call_target="tpu_custom_call" | custom-call | tf_op jit(solution)/shard_map/window_attention/pallas_call | solution.py:475
  127.2 1.3 convert_reduce_fusion
  128.9 15.8 %fusion.24.rows = bf16[512,1024]{1,0:T(8,128)(2,1)} fusion(bf16[512,1024]{1,0:T(8,128)(2,1)S(1)} %get-tuple-element.47, bf16[4096,1024]{1,0:T(8,128)(2,1)} %get-tuple-element.35, bf16[1024,4096]{1,0:T(8,128)(2,1)} %get-tuple-element.34, f32[512]{0:T(512)S(1)} %add_rsqrt_fusion, f32[512]{0:T(512)S(1)} %broadcast_multiply_fusion), kind=kOutput, calls=%fused_computation.33 | convolution fusion | flops 8612478976 | bytes 18878464 | tf_op jit(solution)/shard_map/dot_general | solution.py:640
  144.8 41.5 %final_tables.1 = (f32[6144,8,128]{2,1,0:T(8,128)}, bf16[1024,512]{1,0:T(8,128)(2,1)}) custom-call(bf16[512,1024]{1,0:T(8,128)(2,1)} %fusion.24.rows, bf16[1024,512]{1,0:T(8,128)(2,1)} %wk.1, bf16[1024,512]{1,0:T(8,128)(2,1)} %wv.1), custom_call_target="tpu_custom_call" | custom-call | tf_op jit(solution)/shard_map/final_tables/pallas_call | solution.py:350
  186.7 1.3 reshape.100.idx
  188.0 0.9 constant_dynamic-slice_fusion.gs
  188.9 1.3 copy.29.cnt
  190.2 39.4 %dec_attention.1 = bf16[2048,100]{1,0:T(8,128)(2,1)} custom-call(s32[8192]{0:T(1024)} %reshape.100.idx, f32[6144,8,128]{2,1,0:T(8,128)} %get-tuple-element.36.table, s32[2048,1]{1,0:T(8,128)} %copy.29.cnt, bf16[2048,128]{1,0:T(8,128)(2,1)} %constant_dynamic-slice_fusion.gs, bf16[128,1024]{1,0:T(8,128)(2,1)} %get-tuple-element.37.wq, ...), custom_call_target="tpu_custom_call" | custom-call | tf_op jit(solution)/shard_map/dec_attention/pallas_call | solution.py:564
  229.6 2.1 copy.30
  231.7 1.0 copy.32
  (63 shorter events, 2.5 us)
Async XLA Ops:
  0.6 41.4 %copy-start = (s32[1024,32]{0,1:T(8,128)S(1)}, s32[1024,32]{0,1:T(8,128)}, u32[]{:S(2)}) copy-start(s32[1024,32]{0,1:T(8,128)} %param.22) | copy-start | bytes 393220
  0.6 3.0 %copy-start.15 = (bf16[512,100]{0,1:T(8,128)(2,1)S(1)}, bf16[512,100]{0,1:T(8,128)(2,1)}, u32[]{:S(2)}) copy-start(bf16[512,100]{0,1:T(8,128)(2,1)} %param.39) | copy-start | bytes 307204
  0.7 3.9 %copy-start.16 = (bf16[100,512]{1,0:T(8,128)(2,1)S(1)}, bf16[100,512]{1,0:T(8,128)(2,1)}, u32[]{:S(2)}) copy-start(bf16[100,512]{1,0:T(8,128)(2,1)} %param.26) | copy-start | bytes 307204
  0.7 4.5 %copy-start.17 = (bf16[100,512]{1,0:T(8,128)(2,1)S(1)}, bf16[100,512]{1,0:T(8,128)(2,1)}, u32[]{:S(2)}) copy-start(bf16[100,512]{1,0:T(8,128)(2,1)} %param.27) | copy-start | bytes 307204
  0.7 5.2 %copy-start.18 = (bf16[100,512]{1,0:T(8,128)(2,1)S(1)}, bf16[100,512]{1,0:T(8,128)(2,1)}, u32[]{:S(2)}) copy-start(bf16[100,512]{1,0:T(8,128)(2,1)} %param.36) | copy-start | bytes 307204
  2.4 30.3 %copy-start.10 = (bf16[4096,100]{1,0:T(8,128)(2,1)}, bf16[4096,100]{1,0:T(8,128)(2,1)S(1)}, u32[]{:S(2)}) copy-start(bf16[4096,100]{1,0:T(8,128)(2,1)S(1)} %copy.26) | copy-start | bytes 2457604
  32.7 3.2 %copy-start.12 = (bf16[512,1024]{1,0:T(8,128)(2,1)S(1)}, bf16[512,1024]{1,0:T(8,128)(2,1)}, u32[]{:S(2)}) copy-start(bf16[512,1024]{1,0:T(8,128)(2,1)} %get-tuple-element.21) | copy-start | bytes 3145732
  35.9 4.1 %copy-start.20 = (s32[1024]{0:T(1024)S(1)}, s32[1024]{0:T(1024)}, u32[]{:S(2)}) copy-start(s32[1024]{0:T(1024)} %param.23) | copy-start | bytes 12292
  35.9 8.1 %copy-start.2 = (bf16[4096,128]{1,0:T(8,128)(2,1)S(1)}, bf16[4096,128]{1,0:T(8,128)(2,1)}, u32[]{:S(2)}) copy-start(bf16[4096,128]{1,0:T(8,128)(2,1)} %pad.18.refs_0_.go) | copy-start | bytes 3145732
  35.9 8.1 %copy-start.6 = (bf16[8192,128]{1,0:T(8,128)(2,1)S(1)}, bf16[8192,128]{1,0:T(8,128)(2,1)}, u32[]{:S(2)}) copy-start(bf16[8192,128]{1,0:T(8,128)(2,1)} %get-tuple-element.25.near) | copy-start | bytes 6291460
  44.0 1.0 copy-start.7
  45.0 0.9 copy-start.8
  45.9 1.2 copy-start.9
  47.1 34.7 %copy-start.13 = (bf16[512,1024]{1,0:T(8,128)(2,1)S(1)}, bf16[512,1024]{1,0:T(8,128)(2,1)}, u32[]{:S(2)}) copy-start(bf16[512,1024]{1,0:T(8,128)(2,1)} %get-tuple-element.21) | copy-start | bytes 3145732
  47.1 34.7 %copy-start.22 = (bf16[1024,1024]{1,0:T(8,128)(2,1)S(1)}, bf16[1024,1024]{1,0:T(8,128)(2,1)}, u32[]{:S(2)}) copy-start(bf16[1024,1024]{1,0:T(8,128)(2,1)} %get-tuple-element.26) | copy-start | bytes 6291460
  81.9 2.1 copy-start.5
  83.2 1.7 copy-start.4
  109.4 2.0 copy-start.3
  111.4 15.8 %copy-start.21 = (bf16[1024,1024]{1,0:T(8,128)(2,1)S(1)}, bf16[1024,1024]{1,0:T(8,128)(2,1)}, u32[]{:S(2)}) copy-start(bf16[1024,1024]{1,0:T(8,128)(2,1)} %get-tuple-element.33) | copy-start | bytes 6291460
  144.8 41.6 %copy-start.19 = (s32[4096,4]{0,1:T(4,128)S(1)}, s32[4096,4]{0,1:T(4,128)}, u32[]{:S(2)}) copy-start(s32[4096,4]{0,1:T(4,128)} %param.24) | copy-start | bytes 196612
  144.8 43.2 %copy-start.11 = (bf16[4096,100]{1,0:T(8,128)(2,1)S(1)}, bf16[4096,100]{1,0:T(8,128)(2,1)}, u32[]{:S(2)}) copy-start(bf16[4096,100]{1,0:T(8,128)(2,1)} %copy-done.10) | copy-start | bytes 2457604
  186.3 2.6 %dynamic-slice-start = ((s32[4096]{0:T(1024)}, s32[]{:T(128)}), s32[2048]{0:T(1024)S(1)}, s32[]{:S(2)}) async-start(s32[4096]{0:T(1024)} %param.25, s32[]{:T(128)} %select_n.20), calls=%async_computation | async-start | bytes 16896 | tf_op jit(solution)/shard_map/dynamic_slice | solution.py:623
  190.2 41.4 %copy-start.14 = (bf16[1024,512]{1,0:T(8,128)(2,1)S(1)}, bf16[1024,512]{1,0:T(8,128)(2,1)}, u32[]{:S(2)}) copy-start(bf16[1024,512]{1,0:T(8,128)(2,1)} %get-tuple-element.51) | copy-start | bytes 3145732
  190.2 42.4 %copy-start.1 = (s32[1024,32]{0,1:T(8,128)S(1)}, s32[1024,32]{0,1:T(8,128)}, u32[]{:S(2)}) copy-start(s32[1024,32]{0,1:T(8,128)} %param.22) | copy-start | bytes 393220

commit v4 on v3

--- a/solution.py
+++ b/solution.py
@@ -88,35 +88,45 @@
 
 
 def start_kernel(n_pair, dims, *refs):
-    grid, state = refs[0], refs[1]
-    halves = refs[2 : 2 + n_pair]
-    near, whole = refs[2 + n_pair], refs[3 + n_pair]
-    fulls = refs[4 + n_pair : 4 + 2 * n_pair]
-    rest = refs[4 + 2 * n_pair :]
-    state_hold = rest[0]
-    holds = rest[1 : 1 + n_pair]
-    send_sem, recv_sem, load_sem, store_sem = rest[1 + n_pair :]
+    grid, state, wq = refs[:3]
+    halves = refs[3 : 3 + n_pair]
+    near, whole_out, query = refs[3 + n_pair : 6 + n_pair]
+    fulls = refs[6 + n_pair : 6 + 2 * n_pair]
+    rest = refs[6 + 2 * n_pair :]
+    whole, hold_q = rest[:2]
+    holds = rest[2 : 2 + n_pair]
+    send_sem, recv_sem, load_sem, store_sem = rest[2 + n_pair :]
     band, head, left, right = places()
     peer = (band, 1 - head)
-    loads = [pltpu.make_async_copy(half_of(state, 0, head), state_hold, load_sem.at[n_pair])]
-    loads += [pltpu.make_async_copy(h, v, load_sem.at[n]) for n, (h, v) in enumerate(zip(halves, holds))]
-    for load in loads:
+    early = [pltpu.make_async_copy(half_of(state, 0, head), half_of(whole, 1, head), load_sem.at[n_pair]),
+             pltpu.make_async_copy(wq, half_of(hold_q, 1, head), load_sem.at[n_pair + 1])]
+    loads = [pltpu.make_async_copy(h, v, load_sem.at[n]) for n, (h, v) in enumerate(zip(halves, holds))]
+    for load in early + loads:
         load.start()
     greet([peer, (left, head), (right, head)])
     sender = Sender(send_sem, recv_sem)
     waves = relay(near, lambda own, c, step: grid.at[own], grid.shape[0], (0, 1), sender, None, band, left, right, head, 4)
-    sender.send(half_of(state, 0, 1 - head), half_of(whole, 1, head), peer)
+    first = [sender.send(half_of(state, 0, 1 - head), half_of(whole, 1, head), peer),
+             sender.send(wq, half_of(hold_q, 1, head), peer)]
     for n in range(n_pair):
         sender.send(halves[n], half_of(fulls[n], dims[n], head), peer)
-    stores = [pltpu.make_async_copy(state_hold, half_of(whole, 1, head), store_sem.at[n_pair])]
-    stores += [pltpu.make_async_copy(holds[n], half_of(fulls[n], dims[n], head), store_sem.at[n]) for n in range(n_pair)]
+    stores = [pltpu.make_async_copy(holds[n], half_of(fulls[n], dims[n], head), store_sem.at[n]) for n in range(n_pair)]
     for load, store in zip(loads, stores):
         load.wait()
         store.start()
+    for load in early:
+        load.wait()
+    for copy in first:
+        copy.wait_recv()
+    block = whole.shape[0] // 2
+    for b in range(2):
+        x = whole[b * block:(b + 1) * block, :]
+        whole_out[b * block:(b + 1) * block, :] = x
+        query[b * block:(b + 1) * block, :] = project(layer_norm(x), hold_q[...])
     for copy, rows in waves:
         copy.wait_recv()
         sender.send(near.at[rows], near.at[rows], peer)
-    sender.finish([copy for copy, _ in waves])
+    sender.finish([copy for copy, _ in waves] + first)
     for store in stores:
         store.wait()
 
@@ -127,27 +137,27 @@
     return jax.ShapeDtypeStruct(tuple(shape), half.dtype)
 
 
-def start_exchange(grid, state, pairs):
+def start_exchange(grid, state, wq, pairs):
     halves = [half for half, _ in pairs]
     dims = [dim for _, dim in pairs]
     n = len(pairs)
     nodes, width = state.shape
-    outs = [jax.ShapeDtypeStruct((2 * grid.shape[0], grid.shape[1]), grid.dtype),
-            jax.ShapeDtypeStruct((nodes // 2, width * 2), state.dtype)]
+    rows = jax.ShapeDtypeStruct((nodes // 2, width * 2), state.dtype)
+    outs = [jax.ShapeDtypeStruct((2 * grid.shape[0], grid.shape[1]), grid.dtype), rows, rows]
     outs += [full_shape(half, dim) for half, dim in pairs]
-    copies = 16 + 1 + n
+    copies = 16 + 2 + n
     return pl.pallas_call(
         functools.partial(start_kernel, n, dims),
         out_shape=outs,
-        in_specs=[VM] + [ANY] * (n + 1),
-        out_specs=[ANY] * (n + 2),
-        scratch_shapes=[pltpu.VMEM((nodes // 2, width), state.dtype)]
+        in_specs=[VM] + [ANY] * (n + 2),
+        out_specs=[ANY, VM, VM] + [ANY] * n,
+        scratch_shapes=[pltpu.VMEM(rows.shape, state.dtype), pltpu.VMEM(full_shape(wq, 1).shape, wq.dtype)]
         + [pltpu.VMEM(half.shape, half.dtype) for half in halves]
         + [pltpu.SemaphoreType.DMA((copies,))] * 2
-        + [pltpu.SemaphoreType.DMA((n + 1,))] * 2,
+        + [pltpu.SemaphoreType.DMA((n + 2,)), pltpu.SemaphoreType.DMA((n,))],
         compiler_params=pltpu.CompilerParams(collective_id=0, has_side_effects=True, vmem_limit_bytes=60 << 20),
         name="start_exchange",
-    )(grid, state, *halves)
+    )(grid, state, wq, *halves)
 
 
 def span_kernel(n_pair, dims, *refs):
@@ -244,16 +254,19 @@
     )(rows, wq, wk, wv, *halves)
 
 
-def tables_kernel(rows, wk, wv, table, out, near, hold_k, hold_v, blocks, send_sem, recv_sem, load_sem, store_sem):
+def tables_kernel(att, up, down, wk, wv, table, out, rows, inner, near, hold_u, hold_d, hold_k, hold_v, blocks,
+                  send_sem, recv_sem, load_sem, store_sem):
     band, head, left, right = places()
     count, width = rows.shape
     chunks = 4
     step = count // chunks
+    block = count // 2
     peer = (band, 1 - head)
     lines = blocks.reshape(blocks.shape[0] * blocks.shape[1] * blocks.shape[2] * 8, 128)
+    feeds = [pltpu.make_async_copy(up, hold_u, load_sem.at[2]), pltpu.make_async_copy(down, hold_d, load_sem.at[3])]
     loads = [pltpu.make_async_copy(half, half_of(hold, 1, head), load_sem.at[n])
              for n, (half, hold) in enumerate(((wk, hold_k), (wv, hold_v)))]
-    for load in loads:
+    for load in feeds + loads:
         load.start()
     greet([peer, (left, head), (right, head)])
 
@@ -273,21 +286,46 @@
             src_ref=ours, dst_ref=ours, send_sem=send_sem.at[n], recv_sem=recv_sem.at[n],
             device_id=peer, device_id_type=MESH)
 
-    mine = pl.ds(pl.multiple_of(2 * count + head * count, count), count)
+    base = 2 * count + head * count
+    mine = [pl.ds(pl.multiple_of(base + h * block, block), block) for h in range(2)]
     local = [pltpu.make_async_remote_copy(
         src_ref=src, dst_ref=dst, send_sem=send_sem.at[4 * chunks + n], recv_sem=recv_sem.at[4 * chunks + n],
         device_id=peer, device_id_type=MESH)
-        for n, (src, dst) in enumerate(((wk, half_of(hold_k, 1, head)), (wv, half_of(hold_v, 1, head)), (rows, near.at[mine])))]
-    for c in range(chunks):
-        for side in (0, 4):
-            across(c, side).start()
-    for copy in local:
+        for n, (src, dst) in enumerate(((wk, half_of(hold_k, 1, head)), (wv, half_of(hold_v, 1, head)),
+                                        (rows.at[0:block], near.at[mine[0]]), (rows.at[block:], near.at[mine[1]])))]
+    for copy in local[:2]:
         copy.start()
-    near[mine, :] = rows[...]
-    for load in loads:
-        load.wait()
-    for copy in local:
-        copy.wait_recv()
+
+    def send_half(h):
+        for c in range(h * chunks // 2, (h + 1) * chunks // 2):
+            for side in (0, 4):
+                across(c, side).start()
+        local[2 + h].start()
+
+    feeds[0].wait()
+    part = up.shape[1] // 8
+    for h in range(2):
+        x = att[h * block:(h + 1) * block, :]
+        xn = layer_norm(x)
+        if h == 1:
+            send_half(0)
+
+        def rise(n, carry):
+            for m in range(2):
+                cols = pl.ds(pl.multiple_of((2 * n + m) * part, part), part)
+                up_rows = jnp.dot(xn, hold_u[:, cols], preferred_element_type=jnp.float32)
+                inner[:, cols] = jax.nn.gelu(up_rows, approximate=True).astype(jnp.bfloat16)
+            return carry
+
+        lax.fori_loop(0, 4, rise, 0)
+        if h == 0:
+            feeds[1].wait()
+        for n in range(2):
+            cols = slice(n * width // 2, (n + 1) * width // 2)
+            total = x[:, cols].astype(jnp.float32) + jnp.dot(inner[...], hold_d[:, cols], preferred_element_type=jnp.float32)
+            total = total.astype(jnp.bfloat16)
+            rows[h * block:(h + 1) * block, cols] = total
+            near[mine[h], cols] = total
 
     def stores(base, slot):
         return [pltpu.make_async_copy(
@@ -316,23 +354,32 @@
         for store in stores(base, slot):
             store.start()
 
-    def own(c, carry):
-        project_block(2 * count + c * step, c)
-        return carry
-
-    lax.fori_loop(0, chunks, own, 0)
-    out[...] = near[2 * count:4 * count, pl.ds(pl.multiple_of(head * (width // 2), width // 2), width // 2)]
-
-    def waves(c, carry):
+    for load in loads:
+        load.wait()
+    for copy in local[:2]:
+        copy.wait_recv()
+
+    def own(c, turn):
+        project_block(2 * count + c * step, turn)
+        return turn + 1
+
+    def waves(c, turn):
         for side in (0, 4):
             across(c, side).wait_recv()
             passed(c, side).start()
         for side in (0, 4):
             passed(c, side).wait_recv()
-            project_block(side * count + c * step, chunks + 2 * c + side // 4)
-        return carry
-
-    lax.fori_loop(0, chunks, waves, 0)
+            project_block(side * count + c * step, turn + side // 4)
+        return turn + 2
+
+    local[2].wait_recv()
+    turn = lax.fori_loop(0, 2, own, 0)
+    send_half(1)
+    turn = lax.fori_loop(0, 2, waves, turn)
+    local[3].wait_recv()
+    turn = lax.fori_loop(2, 4, own, turn)
+    out[...] = near[2 * count:4 * count, pl.ds(pl.multiple_of(head * (width // 2), width // 2), width // 2)]
+    lax.fori_loop(2, 4, waves, turn)
     for slot in range(2):
         for store in stores(0, slot):
             store.wait()
@@ -344,33 +391,37 @@
         copy.wait_send()
 
 
-def final_tables(rows, wk, wv):
-    count, width = rows.shape
+def final_tables(att, up, down, wk, wv):
+    count, width = att.shape
     whole = (wk.shape[0], 2 * wk.shape[1])
     return pl.pallas_call(
         tables_kernel,
-        out_shape=[jax.ShapeDtypeStruct((12 * count, 8, 128), jnp.float32), jax.ShapeDtypeStruct((2 * count, width // 2), rows.dtype)],
-        in_specs=[VM, ANY, ANY],
+        out_shape=[jax.ShapeDtypeStruct((12 * count, 8, 128), jnp.float32), jax.ShapeDtypeStruct((2 * count, width // 2), att.dtype)],
+        in_specs=[VM, ANY, ANY, ANY, ANY],
         out_specs=[ANY, VM],
         scratch_shapes=[
-            pltpu.VMEM((6 * count, width), rows.dtype),
+            pltpu.VMEM((count, width), att.dtype),
+            pltpu.VMEM((count // 2, up.shape[1]), att.dtype),
+            pltpu.VMEM((6 * count, width), att.dtype),
+            pltpu.VMEM(up.shape, up.dtype),
+            pltpu.VMEM(down.shape, down.dtype),
             pltpu.VMEM(whole, wk.dtype),
             pltpu.VMEM(whole, wv.dtype),
             pltpu.VMEM((2, 2, count // 2, 8, 128), jnp.float32),
-            pltpu.SemaphoreType.DMA((19,)),
-            pltpu.SemaphoreType.DMA((19,)),
-            pltpu.SemaphoreType.DMA((2,)),
+            pltpu.SemaphoreType.DMA((20,)),
+            pltpu.SemaphoreType.DMA((20,)),
+            pltpu.SemaphoreType.DMA((4,)),
             pltpu.SemaphoreType.DMA((2, 4))],
         compiler_params=pltpu.CompilerParams(collective_id=2, has_side_effects=True, vmem_limit_bytes=60 << 20),
         name="final_tables",
-    )(rows, wk, wv)
+    )(att, up, down, wk, wv)
 
 
 E_ENC = 32
 E_DEC = 4
 
 
-def enc_kernel(idx, q, wk, wv, go, near, bias, out, table, g, qk, mg):
+def enc_kernel(idx, q, wk, wv, go, near, bias, out, table, g_a, g_b, qk, mg):
     i = pl.program_id(0)
     steps = pl.num_programs(0)
     nodes = q.shape[0]
@@ -385,7 +436,7 @@
             @pl.loop(0, band // 128)
             def _(b):
                 r = pl.multiple_of(b * 128, 128)
-                table[pl.ds(part * band + r, 128), 0, :] = ref[pl.ds(r, 128), :].astype(jnp.float32)
+                table[pl.ds(part * band + r, 128), :] = ref[pl.ds(r, 128), :].astype(jnp.float32)
         for c in range(heads2):
             qc = q[:, c * 128:(c + 1) * 128].astype(jnp.float32)
             wc = wk[:, c * 128:(c + 1) * 128]
@@ -395,22 +446,33 @@
                 qk[2 * c + par] = (r * SCALE).astype(jnp.bfloat16)
 
     rows = NB * E_ENC
-    for r in range(rows):
-        g[r:r + 1, :] = table[idx[i * rows + r]]
-    gb = g[...].astype(jnp.bfloat16)
-    n0 = pl.multiple_of(i * NB, NB)
-    qb = qk[:, pl.ds(n0, NB), :].reshape(heads2 * 2 * NB, 128)
-    s = lax.dot_general(qb, gb, (((1,), (1,)), ((), ())), preferred_element_type=jnp.float32)
-    rn = lax.broadcasted_iota(jnp.int32, s.shape, 0) % NB
-    cn = lax.broadcasted_iota(jnp.int32, s.shape, 1) // E_ENC
-    s = jnp.where(rn == cn, s + bias[0], NEGATIVE)
-    p = jnp.exp(s)
-    l = jnp.sum(p, axis=-1, keepdims=True)
-    m = jnp.dot(p.astype(jnp.bfloat16), gb, preferred_element_type=jnp.float32) / l
-    mg[:, pl.ds(n0, NB), :] = m.astype(jnp.bfloat16).reshape(heads2 * 2, NB, 128)
+
+    def gather(block, g):
+        base = block * rows
+        for r in range(rows):
+            g[r:r + 1, :] = table[pl.ds(idx[base + r], 1), :]
+
+    def mixing(block, g):
+        gb = g[...].astype(jnp.bfloat16)
+        n0 = pl.multiple_of(block * NB, NB)
+        qb = qk[:, pl.ds(n0, NB), :].reshape(heads2 * 2 * NB, 128)
+        s = lax.dot_general(qb, gb, (((1,), (1,)), ((), ())), preferred_element_type=jnp.float32)
+        rn = lax.broadcasted_iota(jnp.int32, s.shape, 0) % NB
+        cn = lax.broadcasted_iota(jnp.int32, s.shape, 1) // E_ENC
+        s = jnp.where(rn == cn, s + bias[block], NEGATIVE)
+        p = jnp.exp(s)
+        l = jnp.sum(p, axis=-1, keepdims=True)
+        m = jnp.dot(p.astype(jnp.bfloat16), gb, preferred_element_type=jnp.float32) / l
+        mg[:, pl.ds(n0, NB), :] = m.astype(jnp.bfloat16).reshape(heads2 * 2, NB, 128)
+
+    gather(2 * i, g_a)
+    mixing(jnp.maximum(2 * i - 1, 0), g_b)
+    gather(2 * i + 1, g_b)
+    mixing(2 * i, g_a)
 
     @pl.when(i == steps - 1)
     def _():
+        mixing(2 * i + 1, g_b)
         for c in range(heads2):
             wc = wv[:, c * 128:(c + 1) * 128]
             a = jnp.dot(mg[2 * c], wc, preferred_element_type=jnp.float32)
@@ -428,12 +490,13 @@
         enc_kernel,
         out_shape=jax.ShapeDtypeStruct((nodes, width), jnp.bfloat16),
         grid_spec=pltpu.PrefetchScalarGridSpec(
-            num_scalar_prefetch=1, grid=(steps,),
+            num_scalar_prefetch=1, grid=(steps // 2,),
             in_specs=[full(q), full(wk), full(wv), full(go), full(near),
-                      pl.BlockSpec((1, 1, NB * slots), lambda i, s: (i, 0, 0))],
+                      full(bias)],
             out_specs=pl.BlockSpec((nodes, width), lambda i, s: (0, 0)),
             scratch_shapes=[
-                pltpu.VMEM((3 * go.shape[0], 1, 128), jnp.float32),
+                pltpu.VMEM((3 * go.shape[0], 128), jnp.float32),
+                pltpu.VMEM((NB * slots, 128), jnp.float32),
                 pltpu.VMEM((NB * slots, 128), jnp.float32),
                 pltpu.VMEM((width // 64, nodes, 128), jnp.bfloat16),
                 pltpu.VMEM((width // 64, nodes, 128), jnp.bfloat16)]),
@@ -504,8 +567,9 @@
         qf = jnp.dot(gb, wq[...], preferred_element_type=jnp.float32) * (SCALE * LOG2E)
         for s in range(8):
             q3[:, s] = qf[:, s * 128:(s + 1) * 128].reshape(GB // 8, 8, 128)
+        slots = jnp.broadcast_to(cnt[0].astype(jnp.float32), (128, GB)).T
         for e in range(E_DEC):
-            live[e] = jnp.broadcast_to(jnp.where(cnt[...] > e, 1.0, 0.0), (GB, 128))
+            live[e] = jnp.where(slots > e, 1.0, 0.0)
 
         def gather(o, prod, held):
             base = (g0 + o * UN) * E_DEC
@@ -552,7 +616,7 @@
         o = gb.astype(jnp.float32)
         m2 = jnp.concatenate([mix3[:, s].reshape(GB, 128) for s in range(8)], axis=1).astype(jnp.bfloat16)
         o = o + jnp.dot(m2, wo[...], preferred_element_type=jnp.float32)
-        out[...] = o[:, :out.shape[1]].astype(jnp.bfloat16)
+        out[...] = o.T[:out.shape[0], :].astype(jnp.bfloat16)
 
     work()
 
@@ -563,12 +627,12 @@
     late = lambda i, *_: (i, 0)
     return pl.pallas_call(
         dec_kernel,
-        out_shape=jax.ShapeDtypeStruct((grid_rows, variables), jnp.bfloat16),
+        out_shape=jax.ShapeDtypeStruct((variables, grid_rows), jnp.bfloat16),
         grid_spec=pltpu.PrefetchScalarGridSpec(
             num_scalar_prefetch=1, grid=(steps,),
             in_specs=[full(table),
-                      pl.BlockSpec((GB, 1), late), pl.BlockSpec((GB, 128), late), full(wq), full(wo)],
-            out_specs=pl.BlockSpec((GB, variables), late),
+                      pl.BlockSpec((1, 1, GB), lambda i, *_: (i, 0, 0)), pl.BlockSpec((GB, 128), late), full(wq), full(wo)],
+            out_specs=pl.BlockSpec((variables, GB), lambda i, *_: (0, i)),
             scratch_shapes=[
                 pltpu.VMEM((GB // 8, 8, 8, 128), jnp.float32),
                 pltpu.VMEM((UN, E_DEC // 2, 16, 128), jnp.bfloat16),
@@ -580,7 +644,7 @@
                 pltpu.VMEM((E_DEC, GB, 128), jnp.float32)]),
         compiler_params=pltpu.CompilerParams(dimension_semantics=("arbitrary",), vmem_limit_bytes=60 << 20),
         name="dec_attention",
-    )((sources * 8).reshape(-1), table, counts[:, None], gs, wq, wo)
+    )((sources * 8).reshape(-1), table, counts.reshape(steps, 1, GB), gs, wq, wo)
 
 
 def local(
@@ -614,14 +678,13 @@
     short = 128 - variables
     widen = lambda w: jnp.pad(w, ((0, short), (0, 0)))
     grid = jnp.pad(grid_state, ((0, 0), (0, short)))
-    near_grid, state, enc_k, enc_v, enc_q, enc_o, win_q, win_k, win_v, win_o, dec_q, dec_o = start_exchange(
-        grid, hidden_state,
-        [(widen(encoder_keys), 1), (widen(encoder_values), 1), (encoder_query, 1), (encoder_output, 0),
+    near_grid, state, query, enc_k, enc_v, enc_o, win_q, win_k, win_v, win_o, dec_q, dec_o = start_exchange(
+        grid, hidden_state, encoder_query,
+        [(widen(encoder_keys), 1), (widen(encoder_values), 1), (encoder_output, 0),
          (window_query, 1), (window_keys, 1), (window_values, 1), (window_output, 0),
          (widen(decoder_query), 1), (jnp.pad(decoder_output, ((0, 0), (0, short))), 0)],
     )
     my_rows = lambda a, size: lax.dynamic_slice_in_dim(a, head * size, size, 0)
-    query = project(layer_norm(state), enc_q)
     mix = enc_attention(query, enc_k, enc_v, grid, near_grid, my_rows(encoder_sources, nodes), my_rows(encoder_counts, nodes))
     mid = (state.astype(jnp.float32) + jnp.dot(mix, enc_o, preferred_element_type=jnp.float32)).astype(jnp.bfloat16)
     normed = layer_norm(mid)
@@ -634,14 +697,10 @@
     ones = jnp.broadcast_to(live, (span_rows, 128)).astype(jnp.bfloat16)
     mixed = window(query, keys, values, ones)
     att = (mid.astype(jnp.float32) + jnp.dot(mixed, win_o, preferred_element_type=jnp.float32)).astype(jnp.bfloat16)
-    inner = jax.nn.gelu(
-        jnp.dot(layer_norm(att), up, preferred_element_type=jnp.float32), approximate=True
-    ).astype(jnp.bfloat16)
-    final = (att.astype(jnp.float32) + jnp.dot(inner, down, preferred_element_type=jnp.float32)).astype(jnp.bfloat16)
-    table, hidden_final = final_tables(final, decoder_keys, decoder_values)
+    table, hidden_final = final_tables(att, up, down, decoder_keys, decoder_values)
     sources = my_rows(decoder_sources, half_grid) - (band - 1) * band_nodes
     grid_next = decode(table, my_rows(grid, half_grid), dec_q, dec_o, sources,
-                       my_rows(decoder_counts, half_grid), variables)
+                       my_rows(decoder_counts, half_grid), variables).T
     return (grid_next, hidden_final)
 
 

time: 233 us -> 213 us (0.914)
  matrix products: 22.6 us -> 3.56 us
  other arithmetic: 5.27 us -> 1.58 us
    dot_general x2 -> x0, matrix products: 19.9 us -> none  [the longest x1 15.8 us: local(): jnp.dot(inner, down, preferred_element_type=jnp.float32)]
    pallas_call x1, Pallas kernels: 34.7 us -> 25.5 us  [enc_attention(): pl.pallas_call(enc_kernel, out_shape=jax.ShapeDtypeStruct((nodes, width),...]
    pallas_call x1, Pallas kernels: 41.5 us -> 50.6 us  [final_tables(): pl.pallas_call(tables_kernel, out_shape=[jax.ShapeDtypeStruct((12 * count...]
    pad x3, local copies, waits for them, and re-layouts: 1.98 us -> 4.67 us  [local(): widen = lambda w: jnp.pad(w, ((0, short), (0, 0)))]
    unnamed x50 -> x33, local copies, waits for them, and re-layouts: 10.9 us -> 10.3 us
where the time goes in v4:
time: 213 us; the launch traced here: 212 us
  Pallas kernels  184 us (86%)
  local copies, waits for them, and re-layouts  22.4 us (11%)
  matrix products  3.56 us (2%)
    pallas_call x1, Pallas kernels, final_tables(): pl.pallas_call(tables_kernel, out_shape=[jax.ShapeDtypeStruct((12 * count...  50.6 us
    pallas_call x1, Pallas kernels, decode(): pl.pallas_call(dec_kernel, out_shape=jax.ShapeDtypeStruct((variables, gri...  40.2 us
    pallas_call x1, Pallas kernels, start_exchange(): pl.pallas_call(functools.partial(start_kernel, n, dims), out_shape=outs,...  27.5 us
    pallas_call x1, Pallas kernels, enc_attention(): pl.pallas_call(enc_kernel, out_shape=jax.ShapeDtypeStruct((nodes, width),...  25.5 us
    pallas_call x1, Pallas kernels, window_span(): pl.pallas_call(functools.partial(span_kernel, n, dims), out_shape=outs, i...  24.3 us
    pallas_call x1, Pallas kernels, window(): pl.pallas_call(win_kernel, out_shape=jax.ShapeDtypeStruct((nodes, width),...  15.5 us
    unnamed x33, local copies, waits for them, and re-layouts  10.3 us
    pad x3, local copies, waits for them, and re-layouts, local(): widen = lambda w: jnp.pad(w, ((0, short), (0, 0)))  4.67 us

profile of v4, /device:TPU:1, one launch (start us, length us, event | category | flops | bytes accessed | tf_op | source)
XLA Modules:
  0.0 212.1 jit_solution(2724638879350158332)
XLA Ops:
  0.7 0.8 dynamic_slice.17
  1.5 1.3 dynamic_slice.18
  2.9 0.8 subtract_multiply_fusion
  3.7 1.6 pad.19.refs_3_
  5.3 1.6 pad.20.refs_4_
  6.8 1.6 pad.21.refs_10_
  8.4 1.0 copy.26
  9.4 0.7 pad.22.refs_11_
  10.5 0.2 lt.64
  10.7 0.3 broadcast_in_dim.20.ones
  11.0 0.4 copy.24
  11.4 1.3 reshape.79.idx
  12.7 0.7 copy.25
  13.3 0.9 constant_dynamic-slice_fusion.gs
  14.3 1.2 pad.18.refs_0_.go
  15.5 27.5 %start_exchange.1 = (bf16[8192,128]{1,0:T(8,128)(2,1)}, bf16[512,1024]{1,0:T(8,128)(2,1)}, bf16[512,1024]{1,0:T(8,128)(2,1)}, bf16[128,1024]{1,0:T(8,128)(2,1)},...) custom-call(bf16[4096,128]{1,0:T(8,128)(2,1)} %pad.18.refs_0_.go, ...), custom_call_target="tpu_custom_call" | custom-call | tf_op jit(solution)/shard_map/start_exchange/pallas_call | solution.py:149
  43.0 1.6 copy-done.6
  44.6 1.2 copy-done.7
  45.8 0.9 copy-done.8
  46.8 0.9 copy-done.9
  47.7 25.5 %enc_attention.1 = bf16[512,1024]{1,0:T(8,128)(2,1)S(1)} custom-call(s32[16384]{0:T(1024)S(1)} %reshape.80.idx, bf16[512,1024]{1,0:T(8,128)(2,1)S(1)} %copy-done.7, bf16[128,1024]{1,0:T(8,128)(2,1)S(1)} %copy-done.8, bf16[128,1024]{1,0:T(8,128)(2,1)S(1)} %copy-done.9, bf16[4096,128]{1,0:T(8,128)(2,1)S(1)} %copy-done.2, bf16[8192,128]{1,0:T(8,128)(2,1)S(1)} %copy-done.6, ...), custom_call_target="tpu_custom_call" | custom-call | flops 4294967296 | bytes 8388608 | tf_op jit(solution)/shard_map/enc_attention/pallas_call | solution.py:489
  73.3 1.3 convert_reduce_fusion
  74.6 0.4 fusion.2
  75.0 0.3 fusion.3.refs_0_
  75.4 0.9 copy-done.4
  76.3 24.3 %window_span.1 = (bf16[512,1024]{1,0:T(8,128)(2,1)S(1)}, bf16[1664,1024]{1,0:T(8,128)(2,1)}, bf16[1664,1024]{1,0:T(8,128)(2,1)}, bf16[1024,4096]{1,0:T(8,128)(2,1)}, bf16[4096,1024]{1,0:T(8,128)(2,1)}) custom-call(bf16[512,1024]{1,0:T(8,128)(2,1)S(1)} %fusion.3.refs_0_, bf16[1024,1024]{1,0:T(8,128)(2,1)S(1)} %copy-done.4, bf16[1024,1024]{1,0:T(8,128)(2,1)S(1)} %copy-done.5, ...), custom_call_target="tpu_custom_call" | custom-call | tf_op jit(solution)/shard_map/window_span/pallas_call | solution.py:242
  100.5 2.0 copy-done.3
  102.5 15.5 %window_attention.1 = bf16[512,1024]{1,0:T(8,128)(2,1)S(1)} custom-call(bf16[512,1024]{1,0:T(8,128)(2,1)S(1)} %get-tuple-element.30.q, bf16[1664,1024]{1,0:T(8,128)(2,1)S(1)} %copy-done.3, bf16[1664,1024]{1,0:T(8,128)(2,1)} %get-tuple-element.32.v, bf16[1664,128]{1,0:T(8,128)(2,1)S(1)} %broadcast_in_dim.20.ones), custom_call_target="tpu_custom_call" | custom-call | tf_op jit(solution)/shard_map/window_attention/pallas_call | solution.py:538
  118.0 2.2 %fusion.4.att = bf16[512,1024]{1,0:T(8,128)(2,1)} fusion(bf16[512,1024]{1,0:T(8,128)(2,1)S(1)} %get-tuple-element.41, bf16[512,1024]{1,0:T(8,128)(2,1)S(1)} %window_attention.1, bf16[1024,1024]{1,0:T(8,128)(2,1)S(1)} %copy-done.12), kind=kOutput, calls=%fused_computation.7 | convolution fusion | flops 1075314688 | bytes 5242880 | tf_op jit(solution)/shard_map/dot_general | solution.py:699
  120.3 50.6 %final_tables.1 = (f32[6144,8,128]{2,1,0:T(8,128)}, bf16[1024,512]{1,0:T(8,128)(2,1)}) custom-call(bf16[512,1024]{1,0:T(8,128)(2,1)} %fusion.4.att, bf16[1024,4096]{1,0:T(8,128)(2,1)} %get-tuple-element.34.up, bf16[4096,1024]{1,0:T(8,128)(2,1)} %get-tuple-element.35.down, bf16[1024,512]{1,0:T(8,128)(2,1)} %wk.1, bf16[1024,512]{1,0:T(8,128)(2,1)} %wv.1), custom_call_target="tpu_custom_call" | custom-call | tf_op jit(solution)/shard_map/final_tables/pallas_call | solution.py:397
  170.9 40.2 %dec_attention.1 = bf16[100,2048]{1,0:T(8,128)(2,1)} custom-call(s32[8192]{0:T(1024)} %reshape.79.idx, f32[6144,8,128]{2,1,0:T(8,128)} %get-tuple-element.36.table, s32[16,1,128]{2,1,0:T(1,128)} %bitcast.7, bf16[2048,128]{1,0:T(8,128)(2,1)} %constant_dynamic-slice_fusion.gs, bf16[128,1024]{1,0:T(8,128)(2,1)} %get-tuple-element.37.wq, ...), custom_call_target="tpu_custom_call" | custom-call | tf_op jit(solution)/shard_map/dec_attention/pallas_call | solution.py:628
  211.1 1.0 copy.29
  (35 shorter events, 0.7 us)
Async XLA Ops:
  0.6 3.1 %copy-start = (s32[1024,32]{0,1:T(8,128)S(1)}, s32[1024,32]{0,1:T(8,128)}, u32[]{:S(2)}) copy-start(s32[1024,32]{0,1:T(8,128)} %param.22) | copy-start | bytes 393220
  9.4 3.2 %copy-start.11 = (bf16[4096,100]{0,1:T(8,128)(2,1)S(1)}, bf16[4096,100]{0,1:T(8,128)(2,1)}, u32[]{:S(2)}) copy-start(bf16[4096,100]{0,1:T(8,128)(2,1)} %param.20) | copy-start | bytes 2457604
  15.5 27.5 %copy-start.2 = (bf16[4096,128]{1,0:T(8,128)(2,1)S(1)}, bf16[4096,128]{1,0:T(8,128)(2,1)}, u32[]{:S(2)}) copy-start(bf16[4096,128]{1,0:T(8,128)(2,1)} %pad.18.refs_0_.go) | copy-start | bytes 3145732
  43.0 1.6 copy-start.6
  44.6 1.2 copy-start.7
  45.8 0.9 copy-start.8
  46.8 0.9 copy-start.9
  47.7 25.5 %copy-start.13 = (bf16[1024,1024]{1,0:T(8,128)(2,1)S(1)}, bf16[1024,1024]{1,0:T(8,128)(2,1)}, u32[]{:S(2)}) copy-start(bf16[1024,1024]{1,0:T(8,128)(2,1)} %get-tuple-element.26) | copy-start | bytes 6291460
  47.7 25.5 %copy-start.14 = (bf16[512,1024]{1,0:T(8,128)(2,1)S(1)}, bf16[512,1024]{1,0:T(8,128)(2,1)}, u32[]{:S(2)}) copy-start(bf16[512,1024]{1,0:T(8,128)(2,1)} %get-tuple-element.21) | copy-start | bytes 3145732
  73.3 2.1 copy-start.5
  74.6 1.7 copy-start.4
  100.5 2.0 copy-start.3
  102.5 15.5 %copy-start.12 = (bf16[1024,1024]{1,0:T(8,128)(2,1)S(1)}, bf16[1024,1024]{1,0:T(8,128)(2,1)}, u32[]{:S(2)}) copy-start(bf16[1024,1024]{1,0:T(8,128)(2,1)} %get-tuple-element.33) | copy-start | bytes 6291460
  170.9 40.2 %copy-start.10 = (bf16[1024,512]{1,0:T(8,128)(2,1)S(1)}, bf16[1024,512]{1,0:T(8,128)(2,1)}, u32[]{:S(2)}) copy-start(bf16[1024,512]{1,0:T(8,128)(2,1)} %get-tuple-element.45) | copy-start | bytes 3145732
  170.9 41.2 %copy-start.1 = (s32[1024,32]{0,1:T(8,128)S(1)}, s32[1024,32]{0,1:T(8,128)}, u32[]{:S(2)}) copy-start(s32[1024,32]{0,1:T(8,128)} %param.22) | copy-start | bytes 393220

commit v5 on v4

--- a/solution.py
+++ b/solution.py
@@ -421,7 +421,7 @@
 E_DEC = 4
 
 
-def enc_kernel(idx, q, wk, wv, go, near, bias, out, table, g_a, g_b, qk, mg):
+def enc_kernel(idx, q, wk, wv, go, near, bias, out, table, g_a, g_b, qk, mg, wk_pad, wv_pad):
     i = pl.program_id(0)
     steps = pl.num_programs(0)
     nodes = q.shape[0]
@@ -437,9 +437,12 @@
             def _(b):
                 r = pl.multiple_of(b * 128, 128)
                 table[pl.ds(part * band + r, 128), :] = ref[pl.ds(r, 128), :].astype(jnp.float32)
+        for pad, small in ((wk_pad, wk), (wv_pad, wv)):
+            pad[...] = jnp.zeros_like(pad)
+            pad[0:small.shape[0], :] = small[...]
         for c in range(heads2):
             qc = q[:, c * 128:(c + 1) * 128].astype(jnp.float32)
-            wc = wk[:, c * 128:(c + 1) * 128]
+            wc = wk_pad[:, c * 128:(c + 1) * 128]
             for par in range(2):
                 qm = jnp.where(low if par == 0 else ~low, qc, 0.0).astype(jnp.bfloat16)
                 r = lax.dot_general(qm, wc, (((1,), (1,)), ((), ())), preferred_element_type=jnp.float32)
@@ -474,7 +477,7 @@
     def _():
         mixing(2 * i + 1, g_b)
         for c in range(heads2):
-            wc = wv[:, c * 128:(c + 1) * 128]
+            wc = wv_pad[:, c * 128:(c + 1) * 128]
             a = jnp.dot(mg[2 * c], wc, preferred_element_type=jnp.float32)
             b = jnp.dot(mg[2 * c + 1], wc, preferred_element_type=jnp.float32)
             out[:, c * 128:(c + 1) * 128] = jnp.where(low, a, b).astype(jnp.bfloat16)
@@ -499,7 +502,9 @@
                 pltpu.VMEM((NB * slots, 128), jnp.float32),
                 pltpu.VMEM((NB * slots, 128), jnp.float32),
                 pltpu.VMEM((width // 64, nodes, 128), jnp.bfloat16),
-                pltpu.VMEM((width // 64, nodes, 128), jnp.bfloat16)]),
+                pltpu.VMEM((width // 64, nodes, 128), jnp.bfloat16),
+                pltpu.VMEM((128, width), jnp.bfloat16),
+                pltpu.VMEM((128, width), jnp.bfloat16)]),
         compiler_params=pltpu.CompilerParams(dimension_semantics=("arbitrary",), vmem_limit_bytes=48 << 20),
         cost_estimate=pl.CostEstimate(flops=4 << 30, bytes_accessed=8 << 20, transcendentals=4 << 20),
         name="enc_attention",
@@ -546,7 +551,7 @@
         name="window_attention")(q, k, v, ones)
 
 
-def dec_kernel(idx, table, cnt, gs, wq, wo, out, q3, prod_a, held_a, prod_b, held_b, mix3, seg, live):
+def dec_kernel(idx, table, cnt, gs, wq, wo, out, q3, prod_a, held_a, prod_b, held_b, mix3, seg, live, wq_pad):
     i = pl.program_id(0)
     rows = table.shape[0] // 2
     lines = table.reshape(table.shape[0] * 8, 128)
@@ -560,11 +565,13 @@
         r = lax.broadcasted_iota(jnp.int32, (128, 128), 0) // 64
         c = lax.broadcasted_iota(jnp.int32, (128, 128), 1) // 64
         seg[...] = jnp.where(r == c, 1.0, 0.0).astype(jnp.bfloat16)
+        wq_pad[...] = jnp.zeros_like(wq_pad)
+        wq_pad[0:wq.shape[0], :] = wq[...]
 
     def work():
         g0 = i * GB
         gb = gs[...]
-        qf = jnp.dot(gb, wq[...], preferred_element_type=jnp.float32) * (SCALE * LOG2E)
+        qf = jnp.dot(gb, wq_pad[...], preferred_element_type=jnp.float32) * (SCALE * LOG2E)
         for s in range(8):
             q3[:, s] = qf[:, s * 128:(s + 1) * 128].reshape(GB // 8, 8, 128)
         slots = jnp.broadcast_to(cnt[0].astype(jnp.float32), (128, GB)).T
@@ -613,10 +620,10 @@
         gather(rounds - 1, prod_b, held_b)
         mixing(rounds - 2, prod_a, held_a)
         mixing(rounds - 1, prod_b, held_b)
-        o = gb.astype(jnp.float32)
         m2 = jnp.concatenate([mix3[:, s].reshape(GB, 128) for s in range(8)], axis=1).astype(jnp.bfloat16)
-        o = o + jnp.dot(m2, wo[...], preferred_element_type=jnp.float32)
-        out[...] = o.T[:out.shape[0], :].astype(jnp.bfloat16)
+        update = lax.dot_general(wo[...], m2, (((1,), (1,)), ((), ())), preferred_element_type=jnp.float32)
+        old = gb.astype(jnp.float32).T[:out.shape[0], :]
+        out[...] = (old + update).astype(jnp.bfloat16)
 
     work()
 
@@ -641,7 +648,8 @@
                 pltpu.VMEM((UN, E_DEC, 8, 128), jnp.float32),
                 pltpu.VMEM((GB // 8, 8, 8, 128), jnp.float32),
                 pltpu.VMEM((128, 128), jnp.bfloat16),
-                pltpu.VMEM((E_DEC, GB, 128), jnp.float32)]),
+                pltpu.VMEM((E_DEC, GB, 128), jnp.float32),
+                pltpu.VMEM((128, wq.shape[1]), jnp.bfloat16)]),
         compiler_params=pltpu.CompilerParams(dimension_semantics=("arbitrary",), vmem_limit_bytes=60 << 20),
         name="dec_attention",
     )((sources * 8).reshape(-1), table, counts.reshape(steps, 1, GB), gs, wq, wo)
@@ -676,13 +684,12 @@
     grid_count, variables = grid_state.shape
     half_grid = grid_count // 2
     short = 128 - variables
-    widen = lambda w: jnp.pad(w, ((0, short), (0, 0)))
     grid = jnp.pad(grid_state, ((0, 0), (0, short)))
     near_grid, state, query, enc_k, enc_v, enc_o, win_q, win_k, win_v, win_o, dec_q, dec_o = start_exchange(
         grid, hidden_state, encoder_query,
-        [(widen(encoder_keys), 1), (widen(encoder_values), 1), (encoder_output, 0),
+        [(encoder_keys, 1), (encoder_values, 1), (encoder_output, 0),
          (window_query, 1), (window_keys, 1), (window_values, 1), (window_output, 0),
-         (widen(decoder_query), 1), (jnp.pad(decoder_output, ((0, 0), (0, short))), 0)],
+         (decoder_query, 1), (decoder_output.T, 1)],
     )
     my_rows = lambda a, size: lax.dynamic_slice_in_dim(a, head * size, size, 0)
     mix = enc_attention(query, enc_k, enc_v, grid, near_grid, my_rows(encoder_sources, nodes), my_rows(encoder_counts, nodes))

time: 213 us -> 206 us (0.967)
  local copies, waits for them, and re-layouts: 22.4 us -> 16 us
    pad x4 -> x0, local copies, waits for them, and re-layouts: 5.36 us -> none  [the longest x3 4.67 us: local(): widen = lambda w: jnp.pad(w, ((0, short), (0, 0)))]
    unnamed x33 -> x32, local copies, waits for them, and re-layouts: 10.3 us -> 9.2 us
where the time goes in v5:
time: 206 us; the launch traced here: 205 us
  Pallas kernels  183 us (89%)
  local copies, waits for them, and re-layouts  16 us (8%)
  matrix products  3.56 us (2%)
    pallas_call x1, Pallas kernels, final_tables(): pl.pallas_call(tables_kernel, out_shape=[jax.ShapeDtypeStruct((12 * count...  50.6 us
    pallas_call x1, Pallas kernels, decode(): pl.pallas_call(dec_kernel, out_shape=jax.ShapeDtypeStruct((variables, gri...  39.7 us
    pallas_call x1, Pallas kernels, start_exchange(): pl.pallas_call(functools.partial(start_kernel, n, dims), out_shape=outs,...  27.5 us
    pallas_call x1, Pallas kernels, enc_attention(): pl.pallas_call(enc_kernel, out_shape=jax.ShapeDtypeStruct((nodes, width),...  25.5 us
    pallas_call x1, Pallas kernels, window_span(): pl.pallas_call(functools.partial(span_kernel, n, dims), out_shape=outs, i...  24.3 us
    pallas_call x1, Pallas kernels, window(): pl.pallas_call(win_kernel, out_shape=jax.ShapeDtypeStruct((nodes, width),...  15.5 us
    unnamed x32, local copies, waits for them, and re-layouts  9.2 us

profile of v5, /device:TPU:1, one launch (start us, length us, event | category | flops | bytes accessed | tf_op | source)
XLA Modules:
  0.0 205.2 jit_solution(3211100875117567084)
XLA Ops:
  0.7 0.8 dynamic_slice.17
  1.5 1.3 dynamic_slice.18
  2.8 0.1 lt.60
  2.8 0.1 lt.62
  2.9 0.8 subtract_multiply_fusion
  3.8 0.1 copy.25
  3.9 0.1 reshape.80.idx
  4.1 0.1 lt.63
  4.2 0.2 lt.64
  4.4 0.3 broadcast_in_dim.20.ones
  4.7 0.4 copy.23
  5.1 1.2 reshape.79.idx
  6.3 0.7 copy.24
  7.0 0.9 constant_dynamic-slice_fusion.gs
  8.0 1.2 pad.4.refs_0_.go
  9.1 27.5 %start_exchange.1 = (bf16[8192,128]{1,0:T(8,128)(2,1)}, bf16[512,1024]{1,0:T(8,128)(2,1)}, bf16[512,1024]{1,0:T(8,128)(2,1)}, bf16[100,1024]{1,0:T(8,128)(2,1)},...) custom-call(bf16[4096,128]{1,0:T(8,128)(2,1)} %pad.4.refs_0_.go, ...), custom_call_target="tpu_custom_call" | custom-call | tf_op jit(solution)/shard_map/start_exchange/pallas_call | solution.py:149
  36.7 1.6 copy-done.6
  38.3 1.2 copy-done.7
  39.5 0.9 copy-done.8
  40.4 0.9 copy-done.9
  41.4 25.5 %enc_attention.1 = bf16[512,1024]{1,0:T(8,128)(2,1)S(1)} custom-call(s32[16384]{0:T(1024)S(1)} %reshape.80.idx, bf16[512,1024]{1,0:T(8,128)(2,1)S(1)} %copy-done.7, bf16[100,1024]{1,0:T(8,128)(2,1)S(1)} %copy-done.8, bf16[100,1024]{1,0:T(8,128)(2,1)S(1)} %copy-done.9, bf16[4096,128]{1,0:T(8,128)(2,1)S(1)} %copy-done.2, bf16[8192,128]{1,0:T(8,128)(2,1)S(1)} %copy-done.6, ...), custom_call_target="tpu_custom_call" | custom-call | flops 4294967296 | bytes 8388608 | tf_op jit(solution)/shard_map/enc_attention/pallas_call | solution.py:492
  66.9 1.3 convert_reduce_fusion
  68.3 0.4 fusion.2
  68.7 0.3 fusion.3.refs_0_
  69.0 0.9 copy-done.4
  69.9 24.3 %window_span.1 = (bf16[512,1024]{1,0:T(8,128)(2,1)S(1)}, bf16[1664,1024]{1,0:T(8,128)(2,1)}, bf16[1664,1024]{1,0:T(8,128)(2,1)}, bf16[1024,4096]{1,0:T(8,128)(2,1)}, bf16[4096,1024]{1,0:T(8,128)(2,1)}) custom-call(bf16[512,1024]{1,0:T(8,128)(2,1)S(1)} %fusion.3.refs_0_, bf16[1024,1024]{1,0:T(8,128)(2,1)S(1)} %copy-done.4, bf16[1024,1024]{1,0:T(8,128)(2,1)S(1)} %copy-done.5, ...), custom_call_target="tpu_custom_call" | custom-call | tf_op jit(solution)/shard_map/window_span/pallas_call | solution.py:242
  94.2 2.0 copy-done.3
  96.2 15.5 %window_attention.1 = bf16[512,1024]{1,0:T(8,128)(2,1)S(1)} custom-call(bf16[512,1024]{1,0:T(8,128)(2,1)S(1)} %get-tuple-element.30.q, bf16[1664,1024]{1,0:T(8,128)(2,1)S(1)} %copy-done.3, bf16[1664,1024]{1,0:T(8,128)(2,1)} %get-tuple-element.32.v, bf16[1664,128]{1,0:T(8,128)(2,1)S(1)} %broadcast_in_dim.20.ones), custom_call_target="tpu_custom_call" | custom-call | tf_op jit(solution)/shard_map/window_attention/pallas_call | solution.py:543
  111.7 2.2 %fusion.4.att = bf16[512,1024]{1,0:T(8,128)(2,1)} fusion(bf16[512,1024]{1,0:T(8,128)(2,1)S(1)} %get-tuple-element.41, bf16[512,1024]{1,0:T(8,128)(2,1)S(1)} %window_attention.1, bf16[1024,1024]{1,0:T(8,128)(2,1)S(1)} %copy-done.12), kind=kOutput, calls=%fused_computation.7 | convolution fusion | flops 1075314688 | bytes 5242880 | tf_op jit(solution)/shard_map/dot_general | solution.py:706
  113.9 50.6 %final_tables.1 = (f32[6144,8,128]{2,1,0:T(8,128)}, bf16[1024,512]{1,0:T(8,128)(2,1)}) custom-call(bf16[512,1024]{1,0:T(8,128)(2,1)} %fusion.4.att, bf16[1024,4096]{1,0:T(8,128)(2,1)} %get-tuple-element.34.up, bf16[4096,1024]{1,0:T(8,128)(2,1)} %get-tuple-element.35.down, bf16[1024,512]{1,0:T(8,128)(2,1)} %wk.1, bf16[1024,512]{1,0:T(8,128)(2,1)} %wv.1), custom_call_target="tpu_custom_call" | custom-call | tf_op jit(solution)/shard_map/final_tables/pallas_call | solution.py:397
  164.6 39.7 %dec_attention.1 = bf16[100,2048]{1,0:T(8,128)(2,1)} custom-call(s32[8192]{0:T(1024)} %reshape.79.idx, f32[6144,8,128]{2,1,0:T(8,128)} %get-tuple-element.36.table, s32[16,1,128]{2,1,0:T(1,128)} %bitcast.9, bf16[2048,128]{1,0:T(8,128)(2,1)} %constant_dynamic-slice_fusion.gs, bf16[100,1024]{1,0:T(8,128)(2,1)} %get-tuple-element.37.wq, ...), custom_call_target="tpu_custom_call" | custom-call | tf_op jit(solution)/shard_map/dec_attention/pallas_call | solution.py:635
  204.2 1.0 copy.27
  (30 shorter events, 0.2 us)
Async XLA Ops:
  0.6 3.1 %copy-start = (s32[1024,32]{0,1:T(8,128)S(1)}, s32[1024,32]{0,1:T(8,128)}, u32[]{:S(2)}) copy-start(s32[1024,32]{0,1:T(8,128)} %param.22) | copy-start | bytes 393220
  2.9 3.4 %copy-start.11 = (bf16[4096,100]{0,1:T(8,128)(2,1)S(1)}, bf16[4096,100]{0,1:T(8,128)(2,1)}, u32[]{:S(2)}) copy-start(bf16[4096,100]{0,1:T(8,128)(2,1)} %param.20) | copy-start | bytes 2457604
  9.1 27.5 %copy-start.2 = (bf16[4096,128]{1,0:T(8,128)(2,1)S(1)}, bf16[4096,128]{1,0:T(8,128)(2,1)}, u32[]{:S(2)}) copy-start(bf16[4096,128]{1,0:T(8,128)(2,1)} %pad.4.refs_0_.go) | copy-start | bytes 3145732
  36.7 1.6 copy-start.6
  38.3 1.2 copy-start.7
  39.5 0.9 copy-start.8
  40.4 0.9 copy-start.9
  41.4 25.5 %copy-start.13 = (bf16[1024,1024]{1,0:T(8,128)(2,1)S(1)}, bf16[1024,1024]{1,0:T(8,128)(2,1)}, u32[]{:S(2)}) copy-start(bf16[1024,1024]{1,0:T(8,128)(2,1)} %get-tuple-element.26) | copy-start | bytes 6291460
  41.4 25.5 %copy-start.14 = (bf16[512,1024]{1,0:T(8,128)(2,1)S(1)}, bf16[512,1024]{1,0:T(8,128)(2,1)}, u32[]{:S(2)}) copy-start(bf16[512,1024]{1,0:T(8,128)(2,1)} %get-tuple-element.21) | copy-start | bytes 3145732
  66.9 2.1 %copy-start.5 = (bf16[1024,1024]{1,0:T(8,128)(2,1)S(1)}, bf16[1024,1024]{1,0:T(8,128)(2,1)}, u32[]{:S(2)}) copy-start(bf16[1024,1024]{1,0:T(8,128)(2,1)} %get-tuple-element.28.refs_2_) | copy-start | bytes 6291460
  68.3 1.7 copy-start.4
  94.2 2.0 copy-start.3
  96.2 15.5 %copy-start.12 = (bf16[1024,1024]{1,0:T(8,128)(2,1)S(1)}, bf16[1024,1024]{1,0:T(8,128)(2,1)}, u32[]{:S(2)}) copy-start(bf16[1024,1024]{1,0:T(8,128)(2,1)} %get-tuple-element.33) | copy-start | bytes 6291460
  164.6 39.7 %copy-start.10 = (bf16[1024,512]{1,0:T(8,128)(2,1)S(1)}, bf16[1024,512]{1,0:T(8,128)(2,1)}, u32[]{:S(2)}) copy-start(bf16[1024,512]{1,0:T(8,128)(2,1)} %get-tuple-element.45) | copy-start | bytes 3145732
  164.6 40.6 %copy-start.1 = (s32[1024,32]{0,1:T(8,128)S(1)}, s32[1024,32]{0,1:T(8,128)}, u32[]{:S(2)}) copy-start(s32[1024,32]{0,1:T(8,128)} %param.22) | copy-start | bytes 393220
